TPU v7x, 128 devices: a whole 4x4x4 slice. The times are simulated.
128 devices in a mesh: gx: 8 (over y_hi, z), gy: 16 (over y_lo, x, core).
Axes of the slice: x: 4, y: 4 (y_hi: 2, y_lo: 2; y = y_hi * 2 + y_lo), z: 4, core: 2. Of those that a mesh axis runs over, the one named last changes fastest.
Arguments:
- basis3: float32 [262144, 256], P(('gx', 'gy')), may hold values from -0.046875 to 0.046875
- basis2: float32 [262144, 256], P(('gx', 'gy')), may hold values from -0.03125 to 0.03125
- basis1: float32 [262144, 256], P(('gx', 'gy')), may hold values from -0.0234375 to 0.0234375
- leaf_inverse: float32 [262144], P(('gx', 'gy')), may hold values from 0.25 to 4
- rhs: float32 [262144, 256], P(('gx', 'gy')), may hold values from -6 to 6
- coupling3: float32 [4, 512, 512], replicated, may hold values from -1.5 to 1.5
- coupling2: float32 [2, 512, 512], replicated, may hold values from -1.5 to 1.5
- coupling1: float32 [1, 512, 512], replicated, may hold values from -1.5 to 1.5
Outputs:
- solution: float32 [262144, 256], P(('gx', 'gy'))
- core3: float32 [2048, 512], P(('gx', 'gy'))
- core2: float32 [1024, 512], P(('gx', 'gy'))
- core1: float32 [512, 512], P(('gx', 'gy'))
All inputs are finite; a program needn't handle non-finite values.
Results may differ from a plain program's by a relative error of at most 0.0003.
Values sent between devices are 32-bit elements; how exact they have to be, the bound alone decides.
A program may use at most 128 MiB of HBM per device.

v0:
```python
import jax
import jax.numpy as jnp
from jax import lax
from jax.sharding import PartitionSpec as P

highest_precision = lax.Precision.HIGHEST


def swapped(value, axis, apart):
    mask = 2**apart
    pairs = [(source, source ^ mask) for source in range(lax.axis_size(axis))]
    return lax.ppermute(value, axis, pairs)


def core_solve(coupling_full, gram_upper, gram_lower):
    basis_rank = gram_upper.shape[0]
    upper_rows = coupling_full[:basis_rank]
    lower_rows = coupling_full[basis_rank:]
    inner = jnp.dot(
        upper_rows.T,
        jnp.dot(
            gram_upper, upper_rows, precision=highest_precision, preferred_element_type=jnp.float32
        ),
        precision=highest_precision,
        preferred_element_type=jnp.float32,
    )
    inner = inner + jnp.dot(
        lower_rows.T,
        jnp.dot(
            gram_lower, lower_rows, precision=highest_precision, preferred_element_type=jnp.float32
        ),
        precision=highest_precision,
        preferred_element_type=jnp.float32,
    )
    inner = 0.5 * (inner + inner.T) + jnp.eye(2 * basis_rank, dtype=jnp.float32)
    factor = jnp.linalg.cholesky(inner)
    half_solve = lax.linalg.triangular_solve(factor, coupling_full.T, left_side=True, lower=True)
    return jnp.dot(
        half_solve.T, half_solve, precision=highest_precision, preferred_element_type=jnp.float32
    )


def doubling_sums(gram_local, low_bits):
    running = gram_local
    for bit_index in range(low_bits):
        running = running + swapped(running, ("gx", "gy"), bit_index)
    sibling = swapped(running, ("gx", "gy"), low_bits)
    return (running, sibling)


def block_grams(gram_local, low_bits):
    result_pair = doubling_sums(gram_local, low_bits)
    return result_pair


def per_device(basis3, basis2, basis1, leaf_inverse, rhs, coupling3, coupling2, coupling1):
    basis_rank = basis3.shape[1]
    devices = lax.axis_size("gx") * lax.axis_size("gy")
    total_bits = devices.bit_length() - 1
    device_place = lax.axis_index("gx") * lax.axis_size("gy") + lax.axis_index("gy")
    solved = jnp.concatenate([basis3, basis2, basis1, rhs], axis=1) * leaf_inverse[:, None]
    core_list = []
    for tree_level, basis_now, coupling_now in (
        (3, basis3, coupling3),
        (2, basis2, coupling2),
        (1, basis1, coupling1),
    ):
        low_bits = total_bits - tree_level
        gram_local = jnp.einsum("nr,nw->rw", basis_now, solved, precision=highest_precision)
        own_sum, sibling = block_grams(gram_local, low_bits)
        block_index = device_place >> low_bits
        side_bit = block_index % 2
        pair_index = block_index // 2
        first_half = side_bit == 0
        coupling_full = lax.dynamic_index_in_dim(coupling_now, pair_index, 0, keepdims=False)
        upper_gram = jnp.where(first_half, own_sum, sibling)
        lower_gram = jnp.where(first_half, sibling, own_sum)
        core_full = core_solve(
            coupling_full, upper_gram[:, :basis_rank], lower_gram[:, :basis_rank]
        )
        stacked = jnp.concatenate([upper_gram[:, basis_rank:], lower_gram[:, basis_rank:]], axis=0)
        own_rows = lax.dynamic_slice_in_dim(core_full, side_bit * basis_rank, basis_rank, 0)
        update = jnp.dot(
            own_rows, stacked, precision=highest_precision, preferred_element_type=jnp.float32
        )
        solved = solved[:, basis_rank:] - jnp.dot(
            solved[:, :basis_rank],
            update,
            precision=highest_precision,
            preferred_element_type=jnp.float32,
        )
        rows_each = 2**tree_level * basis_rank // devices
        offset = device_place * rows_each - pair_index * 2 * basis_rank
        core_list.append(lax.dynamic_slice_in_dim(core_full, offset, rows_each, 0))
    return (solved, core_list[0], core_list[1], core_list[2])


def solution(mesh):
    return jax.shard_map(
        per_device,
        mesh=mesh,
        in_specs=(
            P(("gx", "gy"), None),
            P(("gx", "gy"), None),
            P(("gx", "gy"), None),
            P(("gx", "gy")),
            P(("gx", "gy"), None),
            P(),
            P(),
            P(),
        ),
        out_specs=(
            P(("gx", "gy"), None),
            P(("gx", "gy"), None),
            P(("gx", "gy"), None),
            P(("gx", "gy"), None),
        ),
        check_vma=False,
    )
```

profile of v0, /device:TPU:1, one launch (start us, length us, event | category | flops | bytes accessed | tf_op | source)
XLA Modules:
  0.0 845.3 jit_solution(15478207353057223598)
XLA Ops:
  0.6 14.0 %convolution_bitcast_fusion = f32[256,1024]{1,0:T(8,128)S(1)} fusion(f32[2048,256]{1,0:T(8,128)} %param.11, f32[2048,256]{1,0:T(8,128)} %param.15, f32[2048,256]{1,0:T(8,128)} %param.13, f32[2048,256]{1,0:T(8,128)} %param.12, f32[2048]{0:T(1024)} %param.14), kind=kOutput, calls=%fused_computation.23 | convolution fusion | flops 6450839552 | bytes 9445376 | tf_op jit(solution)/shard_map/nr,nw->rw/dot_general | solution.py:69
  19.9 23.0 %collective-permute-done.1 = f32[256,1024]{1,0:T(8,128)S(1)} collective-permute-done((f32[256,1024]{1,0:T(8,128)S(1)}, f32[256,1024]{1,0:T(8,128)S(1)}, u32[]{:S(2)}, u32[]{:S(2)}) %collective-permute-start.1) | collective-permute-done | bytes 1048608 | tf_op jit(solution)/shard_map/ppermute | solution.py:12
  43.1 2.9 collective-permute-start.2
  46.1 22.1 %collective-permute-done.2 = f32[256,1024]{1,0:T(8,128)S(1)} collective-permute-done((f32[256,1024]{1,0:T(8,128)S(1)}, f32[256,1024]{1,0:T(8,128)S(1)}, u32[]{:S(2)}, u32[]{:S(2)}) %collective-permute-start.2) | collective-permute-done | bytes 1048608 | tf_op jit(solution)/shard_map/ppermute | solution.py:12
  69.9 21.2 %collective-permute-done.3 = f32[256,1024]{1,0:T(8,128)S(1)} collective-permute-done((f32[256,1024]{1,0:T(8,128)S(1)}, f32[256,1024]{1,0:T(8,128)S(1)}, u32[]{:S(2)}, u32[]{:S(2)}) %collective-permute-start.3) | collective-permute-done | bytes 1048608 | tf_op jit(solution)/shard_map/ppermute | solution.py:12
  95.4 5.9 maximum_multiply_fusion
  101.3 12.5 %collective-permute-done.4 = f32[256,1024]{1,0:T(8,128)} collective-permute-done((f32[256,1024]{1,0:T(8,128)S(1)}, f32[256,1024]{1,0:T(8,128)}, u32[]{:S(2)}, u32[]{:S(2)}) %collective-permute-start.4) | collective-permute-done | bytes 1048608 | tf_op jit(solution)/shard_map/ppermute | solution.py:12
  128.6 11.7 %cholesky.374 = f32[128,128]{1,0:T(8,128)S(1)} custom-call(f32[128,128]{1,0:T(8,128)S(1)} %cholesky.586), custom_call_target="Cholesky" | custom-call | tf_op jit(solution)/shard_map/jit(cholesky)/cholesky | solution.py:36
  140.5 9.8 %custom-call.31 = f32[1,128,128]{1,2,0:T(8,128)S(1)} custom-call(f32[1,128,128]{2,1,0:T(8,128)S(1)} %get-tuple-element.94), custom_call_target="InvertDiagBlocksLowerTriangular" | custom-call | tf_op jit(solution)/shard_map/jit(cholesky)/cholesky | solution.py:36
  152.8 12.1 %cholesky.393 = f32[128,128]{1,0:T(8,128)S(1)} custom-call(f32[128,128]{1,0:T(8,128)S(1)} %cholesky.590), custom_call_target="Cholesky" | custom-call | tf_op jit(solution)/shard_map/jit(cholesky)/cholesky | solution.py:36
  165.0 9.8 %custom-call.32 = f32[1,128,128]{1,2,0:T(8,128)S(1)} custom-call(f32[1,128,128]{2,1,0:T(8,128)S(1)} %get-tuple-element.91), custom_call_target="InvertDiagBlocksLowerTriangular" | custom-call | tf_op jit(solution)/shard_map/jit(cholesky)/cholesky | solution.py:36
  176.3 11.7 %cholesky.414 = f32[128,128]{1,0:T(8,128)S(1)} custom-call(f32[128,128]{1,0:T(8,128)S(1)} %cholesky.595), custom_call_target="Cholesky" | custom-call | tf_op jit(solution)/shard_map/jit(cholesky)/cholesky | solution.py:36
  188.8 9.8 %custom-call.33 = f32[1,128,128]{1,2,0:T(8,128)S(1)} custom-call(f32[1,128,128]{2,1,0:T(8,128)S(1)} %get-tuple-element.88), custom_call_target="InvertDiagBlocksLowerTriangular" | custom-call | tf_op jit(solution)/shard_map/jit(cholesky)/cholesky | solution.py:36
  200.2 11.7 %cholesky.431 = f32[128,128]{1,0:T(8,128)S(1)} custom-call(f32[128,128]{1,0:T(8,128)S(1)} %convolution_subtract_fusion.18), custom_call_target="Cholesky" | custom-call | tf_op jit(solution)/shard_map/jit(cholesky)/cholesky | solution.py:36
  217.2 11.7 %while.6 = (s32[]{:T(128)}, f32[512,512]{1,0:T(8,128)}, s32[4,2]{0,1:T(2,128)S(1)}, f32[4,128,128]{2,1,0:T(8,128)S(1)}, s32[]{:T(128)}) while((s32[]{:T(128)}, f32[512,512]{1,0:T(8,128)}, s32[4,2]{0,1:T(2,128)S(1)}, f32[4,128,128]{2,1,0:T(8,128)S(1)}, s32[]{:T(128)}) %tuple.79), condition=%wide.while_cond, body=%wide.while_body.sunk | while | flops 2 | bytes 131181 | solution.py:37
  228.9 39.3 %custom-call.34 = f32[4,128,128]{1,2,0:T(8,128)S(1)} custom-call(f32[4,128,128]{2,1,0:T(8,128)S(1)} %get-tuple-element.26), custom_call_target="InvertDiagBlocksLowerTriangular" | custom-call | tf_op jit(solution)/shard_map/triangular_solve/custom-call.3 | solution.py:37
  281.6 10.2 %slice_subtract_fusion = f32[2048,768]{1,0:T(8,128)S(1)} fusion(f32[2048,1024]{1,0:T(8,128)} %maximum_multiply_fusion, f32[256,768]{1,0:T(8,128)S(1)} %fusion.3), kind=kOutput, calls=%fused_computation.7 | convolution fusion | flops 4833411072 | bytes 15466496 | tf_op jit(solution)/shard_map/dot_general | solution.py:86
  291.9 5.7 convolution_bitcast_fusion.1
  297.6 3.6 collective-permute-start.5
  304.5 17.5 %collective-permute-done.6 = f32[256,768]{1,0:T(8,128)S(1)} collective-permute-done((f32[256,768]{1,0:T(8,128)S(1)}, f32[256,768]{1,0:T(8,128)S(1)}, u32[]{:S(2)}, u32[]{:S(2)}) %collective-permute-start.6) | collective-permute-done | bytes 786464 | tf_op jit(solution)/shard_map/ppermute | solution.py:12
  322.1 2.8 collective-permute-start.7
  324.9 16.6 %collective-permute-done.7 = f32[256,768]{1,0:T(8,128)S(1)} collective-permute-done((f32[256,768]{1,0:T(8,128)S(1)}, f32[256,768]{1,0:T(8,128)S(1)}, u32[]{:S(2)}, u32[]{:S(2)}) %collective-permute-start.7) | collective-permute-done | bytes 786464 | tf_op jit(solution)/shard_map/ppermute | solution.py:12
  343.0 15.7 %collective-permute-done.8 = f32[256,768]{1,0:T(8,128)S(1)} collective-permute-done((f32[256,768]{1,0:T(8,128)S(1)}, f32[256,768]{1,0:T(8,128)S(1)}, u32[]{:S(2)}, u32[]{:S(2)}) %collective-permute-start.8) | collective-permute-done | bytes 786464 | tf_op jit(solution)/shard_map/ppermute | solution.py:12
  360.4 14.7 %collective-permute-done.9 = f32[256,768]{1,0:T(8,128)S(1)} collective-permute-done((f32[256,768]{1,0:T(8,128)S(1)}, f32[256,768]{1,0:T(8,128)S(1)}, u32[]{:S(2)}, u32[]{:S(2)}) %collective-permute-start.9) | collective-permute-done | bytes 786464 | tf_op jit(solution)/shard_map/ppermute | solution.py:12
  375.2 3.7 collective-permute-start.10
  379.9 15.7 %collective-permute-done.10 = f32[256,768]{1,0:T(8,128)} collective-permute-done((f32[256,768]{1,0:T(8,128)S(1)}, f32[256,768]{1,0:T(8,128)}, u32[]{:S(2)}, u32[]{:S(2)}) %collective-permute-start.10) | collective-permute-done | bytes 786464 | tf_op jit(solution)/shard_map/ppermute | solution.py:12
  409.8 11.7 %cholesky.446 = f32[128,128]{1,0:T(8,128)S(1)} custom-call(f32[128,128]{1,0:T(8,128)S(1)} %cholesky.599), custom_call_target="Cholesky" | custom-call | tf_op jit(solution)/shard_map/jit(cholesky)/cholesky | solution.py:36
  421.7 9.8 %custom-call.35 = f32[1,128,128]{1,2,0:T(8,128)S(1)} custom-call(f32[1,128,128]{2,1,0:T(8,128)S(1)} %get-tuple-element.84), custom_call_target="InvertDiagBlocksLowerTriangular" | custom-call | tf_op jit(solution)/shard_map/jit(cholesky)/cholesky | solution.py:36
  434.0 12.1 %cholesky.465 = f32[128,128]{1,0:T(8,128)S(1)} custom-call(f32[128,128]{1,0:T(8,128)S(1)} %cholesky.603), custom_call_target="Cholesky" | custom-call | tf_op jit(solution)/shard_map/jit(cholesky)/cholesky | solution.py:36
  447.5 9.8 %custom-call.36 = f32[1,128,128]{1,2,0:T(8,128)S(1)} custom-call(f32[1,128,128]{2,1,0:T(8,128)S(1)} %get-tuple-element.81), custom_call_target="InvertDiagBlocksLowerTriangular" | custom-call | tf_op jit(solution)/shard_map/jit(cholesky)/cholesky | solution.py:36
  458.9 11.7 %cholesky.486 = f32[128,128]{1,0:T(8,128)S(1)} custom-call(f32[128,128]{1,0:T(8,128)S(1)} %cholesky.608), custom_call_target="Cholesky" | custom-call | tf_op jit(solution)/shard_map/jit(cholesky)/cholesky | solution.py:36
  471.3 9.8 %custom-call.37 = f32[1,128,128]{1,2,0:T(8,128)S(1)} custom-call(f32[1,128,128]{2,1,0:T(8,128)S(1)} %get-tuple-element.78), custom_call_target="InvertDiagBlocksLowerTriangular" | custom-call | tf_op jit(solution)/shard_map/jit(cholesky)/cholesky | solution.py:36
  482.7 11.7 %cholesky.503 = f32[128,128]{1,0:T(8,128)S(1)} custom-call(f32[128,128]{1,0:T(8,128)S(1)} %convolution_subtract_fusion.17), custom_call_target="Cholesky" | custom-call | tf_op jit(solution)/shard_map/jit(cholesky)/cholesky | solution.py:36
  499.5 14.3 %while.7 = (s32[]{:T(128)}, f32[512,512]{1,0:T(8,128)}, s32[4,2]{0,1:T(2,128)S(1)}, f32[4,128,128]{2,1,0:T(8,128)}, s32[]{:T(128)}) while((s32[]{:T(128)}, f32[512,512]{1,0:T(8,128)}, s32[4,2]{0,1:T(2,128)S(1)}, f32[4,128,128]{2,1,0:T(8,128)}, s32[]{:T(128)}) %tuple.88), condition=%wide.while_cond.clone, body=%wide.while_body.clone.sunk | while | flops 2 | bytes 132705 | solution.py:37
  500.2 2.9 bitcast_dynamic-update-slice_fusion.7
  503.8 2.9 bitcast_dynamic-update-slice_fusion.7
  507.4 2.9 bitcast_dynamic-update-slice_fusion.7
  511.0 2.9 bitcast_dynamic-update-slice_fusion.7
  513.9 40.2 %custom-call.38 = f32[4,128,128]{1,2,0:T(8,128)S(1)} custom-call(f32[4,128,128]{2,1,0:T(8,128)} %get-tuple-element.27), custom_call_target="InvertDiagBlocksLowerTriangular" | custom-call | tf_op jit(solution)/shard_map/triangular_solve/custom-call.3 | solution.py:37
  566.9 7.9 slice_subtract_fusion.1
  574.9 4.1 convolution_bitcast_fusion.2
  578.9 3.6 collective-permute-start.11
  585.5 11.9 %collective-permute-done.12 = f32[256,512]{1,0:T(8,128)S(1)} collective-permute-done((f32[256,512]{1,0:T(8,128)S(1)}, f32[256,512]{1,0:T(8,128)S(1)}, u32[]{:S(2)}, u32[]{:S(2)}) %collective-permute-start.12) | collective-permute-done | bytes 524320 | tf_op jit(solution)/shard_map/ppermute | solution.py:12
  597.5 2.8 collective-permute-start.13
  600.3 11.0 %collective-permute-done.13 = f32[256,512]{1,0:T(8,128)S(1)} collective-permute-done((f32[256,512]{1,0:T(8,128)S(1)}, f32[256,512]{1,0:T(8,128)S(1)}, u32[]{:S(2)}, u32[]{:S(2)}) %collective-permute-start.13) | collective-permute-done | bytes 524320 | tf_op jit(solution)/shard_map/ppermute | solution.py:12
  612.8 10.1 %collective-permute-done.14 = f32[256,512]{1,0:T(8,128)S(1)} collective-permute-done((f32[256,512]{1,0:T(8,128)S(1)}, f32[256,512]{1,0:T(8,128)S(1)}, u32[]{:S(2)}, u32[]{:S(2)}) %collective-permute-start.14) | collective-permute-done | bytes 524320 | tf_op jit(solution)/shard_map/ppermute | solution.py:12
  623.0 10.5 %collective-permute-done.15 = f32[256,512]{1,0:T(8,128)S(1)} collective-permute-done((f32[256,512]{1,0:T(8,128)S(1)}, f32[256,512]{1,0:T(8,128)S(1)}, u32[]{:S(2)}, u32[]{:S(2)}) %collective-permute-start.15) | collective-permute-done | bytes 524320 | tf_op jit(solution)/shard_map/ppermute | solution.py:12
  635.0 10.3 %collective-permute-done.16 = f32[256,512]{1,0:T(8,128)S(1)} collective-permute-done((f32[256,512]{1,0:T(8,128)S(1)}, f32[256,512]{1,0:T(8,128)S(1)}, u32[]{:S(2)}, u32[]{:S(2)}) %collective-permute-start.16) | collective-permute-done | bytes 524320 | tf_op jit(solution)/shard_map/ppermute | solution.py:12
  646.1 2.9 collective-permute-start.17
  651.9 5.1 collective-permute-done.17
  670.2 11.7 %cholesky.518 = f32[128,128]{1,0:T(8,128)S(1)} custom-call(f32[128,128]{1,0:T(8,128)S(1)} %cholesky.612), custom_call_target="Cholesky" | custom-call | tf_op jit(solution)/shard_map/jit(cholesky)/cholesky | solution.py:36
  683.0 9.8 %custom-call.39 = f32[1,128,128]{1,2,0:T(8,128)S(1)} custom-call(f32[1,128,128]{2,1,0:T(8,128)S(1)} %get-tuple-element.74), custom_call_target="InvertDiagBlocksLowerTriangular" | custom-call | tf_op jit(solution)/shard_map/jit(cholesky)/cholesky | solution.py:36
  696.7 11.9 %cholesky.537 = f32[128,128]{1,0:T(8,128)S(1)} custom-call(f32[128,128]{1,0:T(8,128)S(1)} %cholesky.616), custom_call_target="Cholesky" | custom-call | tf_op jit(solution)/shard_map/jit(cholesky)/cholesky | solution.py:36
  710.6 9.8 %custom-call.40 = f32[1,128,128]{1,2,0:T(8,128)S(1)} custom-call(f32[1,128,128]{2,1,0:T(8,128)S(1)} %get-tuple-element.71), custom_call_target="InvertDiagBlocksLowerTriangular" | custom-call | tf_op jit(solution)/shard_map/jit(cholesky)/cholesky | solution.py:36
  724.3 13.2 %cholesky.558 = f32[128,128]{1,0:T(8,128)} custom-call(f32[128,128]{1,0:T(8,128)} %cholesky.621), custom_call_target="Cholesky" | custom-call | tf_op jit(solution)/shard_map/jit(cholesky)/cholesky | solution.py:36
  739.6 11.3 %custom-call.41 = f32[1,128,128]{1,2,0:T(8,128)} custom-call(f32[1,128,128]{2,1,0:T(8,128)} %get-tuple-element.68), custom_call_target="InvertDiagBlocksLowerTriangular" | custom-call | tf_op jit(solution)/shard_map/jit(cholesky)/cholesky | solution.py:36
  754.2 11.7 %cholesky.575 = f32[128,128]{1,0:T(8,128)S(1)} custom-call(f32[128,128]{1,0:T(8,128)S(1)} %convolution_subtract_fusion.16), custom_call_target="Cholesky" | custom-call | tf_op jit(solution)/shard_map/jit(cholesky)/cholesky | solution.py:36
  772.8 14.2 %while.8 = (s32[]{:T(128)}, f32[512,512]{1,0:T(8,128)}, s32[4,2]{0,1:T(2,128)S(1)}, f32[4,128,128]{2,1,0:T(8,128)}, s32[]{:T(128)}) while((s32[]{:T(128)}, f32[512,512]{1,0:T(8,128)}, s32[4,2]{0,1:T(2,128)S(1)}, f32[4,128,128]{2,1,0:T(8,128)}, s32[]{:T(128)}) %tuple.89), condition=%wide.while_cond.clone.1, body=%wide.while_body.clone.1.sunk | while | flops 2 | bytes 132705 | solution.py:37
  773.5 2.9 bitcast_dynamic-update-slice_fusion.8
  777.0 2.9 bitcast_dynamic-update-slice_fusion.8
  780.6 2.9 bitcast_dynamic-update-slice_fusion.8
  784.1 2.8 bitcast_dynamic-update-slice_fusion.8
  786.9 40.7 %custom-call.42 = f32[4,128,128]{1,2,0:T(8,128)} custom-call(f32[4,128,128]{2,1,0:T(8,128)} %get-tuple-element.28), custom_call_target="InvertDiagBlocksLowerTriangular" | custom-call | tf_op jit(solution)/shard_map/triangular_solve/custom-call.3 | solution.py:37
  841.3 3.2 convolution_subtract_fusion
  (231 shorter events, 168.2 us)
Async XLA Ops:
  0.6 378.2 %copy-start = (f32[2,512,512]{2,1,0:T(8,128)S(1)}, f32[2,512,512]{2,1,0:T(8,128)}, u32[]{:S(2)}) copy-start(f32[2,512,512]{2,1,0:T(8,128)} %param.17) | copy-start | bytes 6291460
  14.6 3.7 collective-permute-start
  18.5 24.4 %collective-permute-start.1 = (f32[256,1024]{1,0:T(8,128)S(1)}, f32[256,1024]{1,0:T(8,128)S(1)}, u32[]{:S(2)}, u32[]{:S(2)}) collective-permute-start(f32[256,1024]{1,0:T(8,128)S(1)} %add.162), channel_id=1, source_target_pairs={{0,2},{1,3},{2,0},{3,1},{4,6},{5,7},{6,4},{7,5},{8,10},{9,11},{10,... | collective-permute-start | bytes 3145736 | tf_op jit(solution)/shard_map/ppermute | solution.py:12
  43.1 52.3 %copy-start.23 = (f32[2048]{0:T(1024)S(1)}, f32[2048]{0:T(1024)}, u32[]{:S(2)}) copy-start(f32[2048]{0:T(1024)} %param.14) | copy-start | bytes 24580
  43.1 25.1 %collective-permute-start.2 = (f32[256,1024]{1,0:T(8,128)S(1)}, f32[256,1024]{1,0:T(8,128)S(1)}, u32[]{:S(2)}, u32[]{:S(2)}) collective-permute-start(f32[256,1024]{1,0:T(8,128)S(1)} %add.163), channel_id=1, source_target_pairs={{0,4},{1,5},{2,6},{3,7},{4,0},{5,1},{6,2},{7,3},{8,12},{9,13},{10,... | collective-permute-start | bytes 3145736 | tf_op jit(solution)/shard_map/ppermute | solution.py:12
  68.4 22.7 %collective-permute-start.3 = (f32[256,1024]{1,0:T(8,128)S(1)}, f32[256,1024]{1,0:T(8,128)S(1)}, u32[]{:S(2)}, u32[]{:S(2)}) collective-permute-start(f32[256,1024]{1,0:T(8,128)S(1)} %add.164), channel_id=1, source_target_pairs={{0,8},{1,9},{2,10},{3,11},{4,12},{5,13},{6,14},{7,15},{8,0},{9,1},... | collective-permute-start | bytes 3145736 | tf_op jit(solution)/shard_map/ppermute | solution.py:12
  91.3 22.5 %collective-permute-start.4 = (f32[256,1024]{1,0:T(8,128)S(1)}, f32[256,1024]{1,0:T(8,128)}, u32[]{:S(2)}, u32[]{:S(2)}) collective-permute-start(f32[256,1024]{1,0:T(8,128)S(1)} %add.165), channel_id=1, source_target_pairs={{0,16},{1,17},{2,18},{3,19},{4,20},{5,21},{6,22},{7,23},{8,24},{9,... | collective-permute-start | bytes 3145736 | tf_op jit(solution)/shard_map/ppermute | solution.py:12
  101.3 14.0 %copy-start.16 = (f32[4,512,512]{2,1,0:T(8,128)S(1)}, f32[4,512,512]{2,1,0:T(8,128)}, u32[]{:S(2)}) copy-start(f32[4,512,512]{2,1,0:T(8,128)} %param.16) | copy-start | bytes 12582916
  120.5 1.0 copy-start.5
  127.5 1.1 copy-start.15
  228.9 51.3 %copy-start.11 = (f32[256,768]{1,0:T(8,128)S(1)}, f32[256,768]{1,0:T(8,128)}, u32[]{:S(2)}) copy-start(f32[256,768]{1,0:T(8,128)} %slice.296) | copy-start | bytes 2359300
  268.2 11.9 %copy-start.12 = (f32[256,768]{1,0:T(8,128)S(1)}, f32[256,768]{1,0:T(8,128)}, u32[]{:S(2)}) copy-start(f32[256,768]{1,0:T(8,128)} %slice.297) | copy-start | bytes 2359300
  279.0 1.1 copy-start.21
  281.6 10.2 %copy-start.10 = (f32[2048,256]{1,0:T(8,128)S(1)}, f32[2048,256]{1,0:T(8,128)}, u32[]{:S(2)}) copy-start(f32[2048,256]{1,0:T(8,128)} %param.12) | copy-start | bytes 6291460
  291.9 5.7 copy-start.1
  297.6 5.5 collective-permute-start.5
  303.2 18.8 %collective-permute-start.6 = (f32[256,768]{1,0:T(8,128)S(1)}, f32[256,768]{1,0:T(8,128)S(1)}, u32[]{:S(2)}, u32[]{:S(2)}) collective-permute-start(f32[256,768]{1,0:T(8,128)S(1)} %add.173), channel_id=1, source_target_pairs={{0,2},{1,3},{2,0},{3,1},{4,6},{5,7},{6,4},{7,5},{8,10},{9,11},{10,... | collective-permute-start | bytes 2359304 | tf_op jit(solution)/shard_map/ppermute | solution.py:12
  322.1 19.5 %collective-permute-start.7 = (f32[256,768]{1,0:T(8,128)S(1)}, f32[256,768]{1,0:T(8,128)S(1)}, u32[]{:S(2)}, u32[]{:S(2)}) collective-permute-start(f32[256,768]{1,0:T(8,128)S(1)} %add.174), channel_id=1, source_target_pairs={{0,4},{1,5},{2,6},{3,7},{4,0},{5,1},{6,2},{7,3},{8,12},{9,13},{10,... | collective-permute-start | bytes 2359304 | tf_op jit(solution)/shard_map/ppermute | solution.py:12
  341.6 17.1 %collective-permute-start.8 = (f32[256,768]{1,0:T(8,128)S(1)}, f32[256,768]{1,0:T(8,128)S(1)}, u32[]{:S(2)}, u32[]{:S(2)}) collective-permute-start(f32[256,768]{1,0:T(8,128)S(1)} %add.175), channel_id=1, source_target_pairs={{0,8},{1,9},{2,10},{3,11},{4,12},{5,13},{6,14},{7,15},{8,0},{9,1},... | collective-permute-start | bytes 2359304 | tf_op jit(solution)/shard_map/ppermute | solution.py:12
  358.8 16.2 %collective-permute-start.9 = (f32[256,768]{1,0:T(8,128)S(1)}, f32[256,768]{1,0:T(8,128)S(1)}, u32[]{:S(2)}, u32[]{:S(2)}) collective-permute-start(f32[256,768]{1,0:T(8,128)S(1)} %add.176), channel_id=1, source_target_pairs={{0,16},{1,17},{2,18},{3,19},{4,20},{5,21},{6,22},{7,23},{8,24},{9,... | collective-permute-start | bytes 2359304 | tf_op jit(solution)/shard_map/ppermute | solution.py:12
  375.2 20.4 %collective-permute-start.10 = (f32[256,768]{1,0:T(8,128)S(1)}, f32[256,768]{1,0:T(8,128)}, u32[]{:S(2)}, u32[]{:S(2)}) collective-permute-start(f32[256,768]{1,0:T(8,128)S(1)} %add.177), channel_id=1, source_target_pairs={{0,32},{1,33},{2,34},{3,35},{4,36},{5,37},{6,38},{7,39},{8,40},{9,... | collective-permute-start | bytes 2359304 | tf_op jit(solution)/shard_map/ppermute | solution.py:12
  401.9 1.0 copy-start.4
  408.8 1.0 copy-start.13
  513.9 52.0 %copy-start.17 = (f32[256,512]{1,0:T(8,128)S(1)}, f32[256,512]{1,0:T(8,128)}, u32[]{:S(2)}) copy-start(f32[256,512]{1,0:T(8,128)} %slice.313) | copy-start | bytes 1572868
  513.9 52.0 %copy-start.18 = (f32[256,512]{1,0:T(8,128)S(1)}, f32[256,512]{1,0:T(8,128)}, u32[]{:S(2)}) copy-start(f32[256,512]{1,0:T(8,128)} %slice.314) | copy-start | bytes 1572868
  564.9 1.0 copy-start.22
  565.8 9.0 %copy-start.9 = (f32[2048,256]{1,0:T(8,128)S(1)}, f32[2048,256]{1,0:T(8,128)}, u32[]{:S(2)}) copy-start(f32[2048,256]{1,0:T(8,128)} %param.13) | copy-start | bytes 6291460
  574.9 9.3 %copy-start.2 = (f32[2048,512]{1,0:T(8,128)}, f32[2048,512]{1,0:T(8,128)S(1)}, u32[]{:S(2)}) copy-start(f32[2048,512]{1,0:T(8,128)S(1)} %slice_subtract_fusion.1) | copy-start | bytes 12582916
  578.9 5.1 collective-permute-start.11
  584.2 13.2 %collective-permute-start.12 = (f32[256,512]{1,0:T(8,128)S(1)}, f32[256,512]{1,0:T(8,128)S(1)}, u32[]{:S(2)}, u32[]{:S(2)}) collective-permute-start(f32[256,512]{1,0:T(8,128)S(1)} %add.184), channel_id=1, source_target_pairs={{0,2},{1,3},{2,0},{3,1},{4,6},{5,7},{6,4},{7,5},{8,10},{9,11},{10,... | collective-permute-start | bytes 1572872 | tf_op jit(solution)/shard_map/ppermute | solution.py:12
  597.4 60.9 %copy-start.6 = (f32[1,512,512]{2,1,0:T(8,128)S(1)}, f32[1,512,512]{2,1,0:T(8,128)}, u32[]{:S(2)}) copy-start(f32[1,512,512]{2,1,0:T(8,128)} %param.18) | copy-start | bytes 3145732
  597.5 13.8 %collective-permute-start.13 = (f32[256,512]{1,0:T(8,128)S(1)}, f32[256,512]{1,0:T(8,128)S(1)}, u32[]{:S(2)}, u32[]{:S(2)}) collective-permute-start(f32[256,512]{1,0:T(8,128)S(1)} %add.185), channel_id=1, source_target_pairs={{0,4},{1,5},{2,6},{3,7},{4,0},{5,1},{6,2},{7,3},{8,12},{9,13},{10,... | collective-permute-start | bytes 1572872 | tf_op jit(solution)/shard_map/ppermute | solution.py:12
  611.4 11.5 %collective-permute-start.14 = (f32[256,512]{1,0:T(8,128)S(1)}, f32[256,512]{1,0:T(8,128)S(1)}, u32[]{:S(2)}, u32[]{:S(2)}) collective-permute-start(f32[256,512]{1,0:T(8,128)S(1)} %add.186), channel_id=1, source_target_pairs={{0,8},{1,9},{2,10},{3,11},{4,12},{5,13},{6,14},{7,15},{8,0},{9,1},... | collective-permute-start | bytes 1572872 | tf_op jit(solution)/shard_map/ppermute | solution.py:12
  622.9 10.6 %collective-permute-start.15 = (f32[256,512]{1,0:T(8,128)S(1)}, f32[256,512]{1,0:T(8,128)S(1)}, u32[]{:S(2)}, u32[]{:S(2)}) collective-permute-start(f32[256,512]{1,0:T(8,128)S(1)} %add.187), channel_id=1, source_target_pairs={{0,16},{1,17},{2,18},{3,19},{4,20},{5,21},{6,22},{7,23},{8,24},{9,... | collective-permute-start | bytes 1572872 | tf_op jit(solution)/shard_map/ppermute | solution.py:12
  633.6 11.6 %collective-permute-start.16 = (f32[256,512]{1,0:T(8,128)S(1)}, f32[256,512]{1,0:T(8,128)S(1)}, u32[]{:S(2)}, u32[]{:S(2)}) collective-permute-start(f32[256,512]{1,0:T(8,128)S(1)} %add.188), channel_id=1, source_target_pairs={{0,32},{1,33},{2,34},{3,35},{4,36},{5,37},{6,38},{7,39},{8,40},{9,... | collective-permute-start | bytes 1572872 | tf_op jit(solution)/shard_map/ppermute | solution.py:12
  646.1 10.8 %collective-permute-start.17 = (f32[256,512]{1,0:T(8,128)}, f32[256,512]{1,0:T(8,128)}, u32[]{:S(2)}, u32[]{:S(2)}) collective-permute-start(f32[256,512]{1,0:T(8,128)} %add.189), channel_id=1, source_target_pairs={{0,64},{1,65},{2,66},{3,67},{4,68},{5,69},{6,70},{7,71},{8,72},{9,... | collective-permute-start | bytes 1572872 | tf_op jit(solution)/shard_map/ppermute | solution.py:12
  649.1 12.3 %copy-start.7 = (f32[1,512,512]{2,1,0:T(8,128)S(1)}, f32[1,512,512]{2,1,0:T(8,128)}, u32[]{:S(2)}) copy-start(f32[1,512,512]{2,1,0:T(8,128)} %param.18) | copy-start | bytes 3145732
  669.2 1.0 copy-start.14
  670.2 157.5 %copy-start.8 = (f32[1,512,512]{2,1,0:T(8,128)S(1)}, f32[1,512,512]{2,1,0:T(8,128)}, u32[]{:S(2)}) copy-start(f32[1,512,512]{2,1,0:T(8,128)} %param.18) | copy-start | bytes 3145732
  696.0 0.7 copy-start.20
  827.7 13.0 %copy-start.19 = (f32[256,256]{1,0:T(8,128)S(1)}, f32[256,256]{1,0:T(8,128)}, u32[]{:S(2)}) copy-start(f32[256,256]{1,0:T(8,128)} %slice.331) | copy-start | bytes 786436
  830.4 10.9 %copy-start.3 = (f32[2048,512]{1,0:T(8,128)S(1)}, f32[2048,512]{1,0:T(8,128)}, u32[]{:S(2)}) copy-start(f32[2048,512]{1,0:T(8,128)} %copy-done.2) | copy-start | bytes 12582916
where the time goes:
time: 857 us; the launch traced here: 845 us
  other arithmetic  391 us (46%)
  waiting for transfers between devices  224 us (26%)
  matrix products  114 us (13%)
  local copies, waits for them, and re-layouts  70.7 us (8%)
  starting transfers between devices  36.8 us (4%)
  between operations  9.51 us (1%)
    another operation x44, other arithmetic, core_solve(): factor = jnp.linalg.cholesky(inner)  243 us
    ppermute x18, waiting for transfers between devices, swapped(): return lax.ppermute(value, axis, pairs)  224 us
    another operation x7, other arithmetic, core_solve(): lax.linalg.triangular_solve(factor, coupling_full.T, left_side=True, lowe...  125 us
    another operation x40, local copies, waits for them, and re-layouts, core_solve(): lax.linalg.triangular_solve(factor, coupling_full.T, left_side=True, lowe...  41.5 us
    ppermute x18, starting transfers between devices, swapped(): return lax.ppermute(value, axis, pairs)  36.8 us
    another operation x21, matrix products, core_solve(): lax.linalg.triangular_solve(factor, coupling_full.T, left_side=True, lowe...  28.7 us
    dot_general x3, matrix products, per_device(): jnp.einsum('nr,nw->rw', basis_now, solved, precision=highest_precision)  23.7 us
    dot_general x3, matrix products, per_device(): jnp.dot(solved[:, :basis_rank], update, precision=highest_precision, pref...  21.3 us
  transfers between devices with their start and end apart: 18, of which 18 were waited for; matrix products, arithmetic and copies ran while one was open for 1% of the time, Pallas kernels for 0%

commit v1 on v0

v1 whole, which is shorter than its diff:
```python
import jax
import jax.numpy as jnp
from jax import lax
from jax.experimental import pallas as pl
from jax.experimental.pallas import tpu as pltpu
from jax.sharding import PartitionSpec as P

F32 = jnp.float32
BF16 = jnp.bfloat16
NN = ((1,), (0,))
TN = ((0,), (0,))
W = 16
NB = 128
VMEM = pl.BlockSpec(memory_space=pltpu.VMEM)


def dot6(a, b, dims):
    return lax.dot_general(
        a, b, (dims, ((), ())), precision=lax.Precision.HIGHEST, preferred_element_type=F32
    )


def dot1(a, b, dims):
    return lax.dot_general(a, b, (dims, ((), ())), preferred_element_type=F32)


def split2(x):
    hi = x.astype(BF16)
    return hi, (x - hi.astype(F32)).astype(BF16)


def split3(x):
    hi = x.astype(BF16)
    rest = x - hi.astype(F32)
    mid = rest.astype(BF16)
    return hi, mid, (rest - mid.astype(F32)).astype(BF16)


def dot3(a, b, dims):
    return dot1(a[0], b[0], dims) + (dot1(a[0], b[1], dims) + dot1(a[1], b[0], dims))


def gram_kernel(b3, b2, b1, rhs, leaf, first, rest):
    @pl.when(pl.program_id(0) == 0)
    def _():
        first[...] = jnp.zeros_like(first)
        rest[...] = jnp.zeros_like(rest)

    root = jnp.sqrt(leaf[...])
    t3, t2, t1, tr = (split2(x[...] * root) for x in (b3, b2, b1, rhs))
    r = b3.shape[1]
    first[...] += dot3(t3, t3, TN)
    at = 0
    for left, rights in ((t3, (t2, t1, tr)), (t2, (t2, t1, tr)), (t1, (t1, tr))):
        for right in rights:
            rest[:, at : at + r] += dot3(left, right, TN)
            at += r


def grams(b3, b2, b1, rhs, leaf):
    rows, r = b3.shape
    tile = 512
    block = pl.BlockSpec((tile, r), lambda i: (i, 0))
    return pl.pallas_call(
        gram_kernel,
        grid=(rows // tile,),
        in_specs=[block] * 4 + [pl.BlockSpec((tile, 1), lambda i: (i, 0))],
        out_specs=[pl.BlockSpec((r, r), lambda i: (0, 0)), pl.BlockSpec((r, 8 * r), lambda i: (0, 0))],
        out_shape=[jax.ShapeDtypeStruct((r, r), F32), jax.ShapeDtypeStruct((r, 8 * r), F32)],
        name="grams",
    )(b3, b2, b1, rhs, leaf[:, None])


def invert_factor(work, cols, rows, panel):
    n = work.shape[0]
    lane = lax.broadcasted_iota(jnp.int32, (W, n), 1)
    sub = lax.broadcasted_iota(jnp.int32, (W, n), 0)
    for s in range(n // W):
        o = s * W
        block = work[o : o + W, :]
        for k in range(W):
            cols[k * W : (k + 1) * W, :] = jnp.broadcast_to(block[:, o + k : o + k + 1], (W, n))
        inside = (lane >= o) & (lane < o + W)
        rows[...] = jnp.where(inside, jnp.where(lane - o == sub, 1.0, 0.0), block)
        c = {(i, k): cols[i * W + k : i * W + k + 1, :] for i in range(W) for k in range(i + 1)}
        x = [rows[i : i + 1, :] for i in range(W)]
        for k in range(W):
            recip = 1.0 / c[k, k]
            for i in range(k + 1, W):
                m = c[i, k] * recip
                for j in range(k + 1, i + 1):
                    c[i, j] = c[i, j] - m * c[j, k]
                x[i] = x[i] - m * x[k]
            panel[k : k + 1, :] = x[k] * lax.rsqrt(c[k, k])
        v = panel[...]
        work[o : o + W, :] = jnp.where(lane < o + W, v, 0.0)
        t = o + W
        if t < n:
            v1, v2, v3 = split3(v)
            left = jnp.concatenate([v1, v1, v2, v1, v3, v2], 0)
            right = jnp.concatenate([v1, v2, v1, v3, v1, v2], 0)
            update = dot1(left, right, TN)
            below = lax.broadcasted_iota(jnp.int32, (n - t, n), 1)
            kept = jnp.where((below >= o) & (below < t), 0.0, work[t:, :])
            work[t:, :] = kept - update[t:, :]


def factor_kernel(g, coupling, m, c, work, cols, rows, panel):
    r = g.shape[1]
    order = 2 * r
    steps = order // NB
    gl = jnp.concatenate(
        [dot6(g[:r, :], coupling[:r, :], NN), dot6(g[r:, :], coupling[r:, :], NN)], 0
    )
    eye = jnp.where(
        lax.broadcasted_iota(jnp.int32, (NB, NB), 0) == lax.broadcasted_iota(jnp.int32, (NB, NB), 1),
        1.0,
        0.0,
    )
    full = coupling[...]
    for j in range(steps):
        o = j * NB
        c[o : o + NB, o:order] = dot6(full[:, o : o + NB], gl[:, o:], TN)
        c[o : o + NB, order:] = full[:, o : o + NB].T

    def step(j, carry):
        for jj in range(steps):

            @pl.when(j == jj)
            def _(o=jj * NB):
                work[...] = c[o : o + NB, o : o + NB] + eye

        invert_factor(work, cols, rows, panel)
        for jj in range(steps):

            @pl.when(j == jj)
            def _(jj=jj, o=jj * NB, t=jj * NB + NB):
                out = dot6(work[...], c[o : o + NB, t:], NN)
                m[o : o + NB, :] = out[:, order - t :]
                for q in range(jj + 1, steps):
                    w = q * NB
                    c[w : w + NB, w:] = c[w : w + NB, w:] - dot6(
                        out[:, w - t : w - t + NB], out[:, w - t :], TN
                    )

        return carry

    lax.fori_loop(0, steps, step, 0)


def factor(g, coupling):
    order = coupling.shape[0]
    return pl.pallas_call(
        factor_kernel,
        out_shape=jax.ShapeDtypeStruct((order, order), F32),
        in_specs=[VMEM] * 2,
        out_specs=VMEM,
        scratch_shapes=[
            pltpu.VMEM((order, 2 * order), F32),
            pltpu.VMEM((NB, NB), F32),
            pltpu.VMEM((W * W, NB), F32),
            pltpu.VMEM((W, NB), F32),
            pltpu.VMEM((W, NB), F32),
        ],
        name="factor",
        cost_estimate=pl.CostEstimate(flops=2_000_000_000, bytes_accessed=3 << 20, transcendentals=0),
    )(g, coupling)


def level_kernel(levels, m, q, sums, half, v, h):
    r = m.shape[0] // 2
    ms = split2(m[...])
    ps = split2(dot3(ms, split2(q[...]), NN))
    own = split2(m[:, pl.ds(pl.multiple_of(half[0] * r, r), r)])
    v[...] = dot3(own, ps, TN)
    at = 0
    for i in range(levels):
        left = tuple(x[:, i * r : (i + 1) * r] for x in ps)
        for j in range(i, levels + 1):
            right = tuple(x[:, j * r : (j + 1) * r] for x in ps)
            h[:, at : at + r] = sums[:, at : at + r] - dot3(left, right, TN)
            at += r


def level_update(levels, m, q, sums, half):
    r = m.shape[0] // 2
    wide = (levels + 1) * r
    return pl.pallas_call(
        lambda *refs: level_kernel(levels, *refs),
        out_shape=[jax.ShapeDtypeStruct((r, wide), F32), jax.ShapeDtypeStruct(sums.shape, F32)],
        in_specs=[VMEM] * 3 + [pl.BlockSpec(memory_space=pltpu.SMEM)],
        out_specs=[VMEM, VMEM],
        name="level_update",
    )(m, q, sums, half)


def back_kernel(m, q, half, v3, v2, x):
    r = m.shape[0] // 2
    ps = dot3(split2(m[...]), split2(q[...]), NN)
    x1 = dot3(split2(m[:, pl.ds(pl.multiple_of(half[0] * r, r), r)]), split2(ps), TN)
    s1 = split2(x1)
    x2 = v2[:, r:] - dot3(split2(v2[:, :r]), s1, NN)
    s2 = split2(x2)
    x3 = v3[:, 2 * r :] - dot3(split2(v3[:, :r]), s2, NN) - dot3(split2(v3[:, r : 2 * r]), s1, NN)
    x[:r, :] = x3
    x[r : 2 * r, :] = x2
    x[2 * r :, :] = x1


def back(m, q, half, v3, v2):
    r = m.shape[0] // 2
    return pl.pallas_call(
        back_kernel,
        out_shape=jax.ShapeDtypeStruct((3 * r, r), F32),
        in_specs=[VMEM] * 2 + [pl.BlockSpec(memory_space=pltpu.SMEM)] + [VMEM] * 2,
        out_specs=VMEM,
        name="back",
    )(m, q, half, v3, v2)


def apply_kernel(b3, b2, b1, rhs, leaf, x, out):
    r = b3.shape[1]
    xs = split2(x[...])
    total = rhs[...]
    for i, b in enumerate((b3, b2, b1)):
        total = total - dot3(split2(b[...]), tuple(y[i * r : (i + 1) * r] for y in xs), NN)
    out[...] = total * leaf[...]


def apply_update(b3, b2, b1, rhs, leaf, x):
    rows, r = b3.shape
    tile = 512
    block = pl.BlockSpec((tile, r), lambda i: (i, 0))
    return pl.pallas_call(
        apply_kernel,
        grid=(rows // tile,),
        in_specs=[block] * 4
        + [pl.BlockSpec((tile, 1), lambda i: (i, 0)), pl.BlockSpec(x.shape, lambda i: (0, 0))],
        out_specs=block,
        out_shape=jax.ShapeDtypeStruct(rhs.shape, F32),
        name="apply_update",
    )(b3, b2, b1, rhs, leaf[:, None], x)


def core_rows(m, offset, count):
    own = lax.dynamic_slice_in_dim(m, offset, count, 1)
    return lax.dot_general(
        own, m, (TN, ((), ())), precision=lax.Precision.HIGHEST, preferred_element_type=F32
    )


def per_device(basis3, basis2, basis1, leaf_inverse, rhs, coupling3, coupling2, coupling1):
    r = basis3.shape[1]
    nx = lax.axis_size("gx")
    ny = lax.axis_size("gy")
    devices = nx * ny
    gx = lax.axis_index("gx")
    place = gx * ny + lax.axis_index("gy")

    def sibling(value, bit):
        return lax.ppermute(value, "gx", [(s, s ^ (1 << bit)) for s in range(nx)])

    def ordered(value, other, bit):
        low = (gx >> bit) & 1 == 0
        return jnp.concatenate(
            [jnp.where(low, value, other), jnp.where(low, other, value)], axis=0
        )

    first, rest = grams(basis3, basis2, basis1, rhs, leaf_inverse)
    first = lax.psum(first, "gy")
    g3 = ordered(first, sibling(first, 0), 0)
    rest = lax.psum(rest, "gy")
    rest_other = sibling(rest, 0)
    q3 = ordered(rest[:, : 3 * r], rest_other[:, : 3 * r], 0)
    sums = rest[:, 3 * r :] + rest_other[:, 3 * r :]

    pair3 = lax.dynamic_index_in_dim(coupling3, gx >> 1, 0, keepdims=False)
    m3 = factor(g3, pair3)
    v3, h2 = level_update(2, m3, q3, sums, (gx & 1).reshape(1))
    h2_other = sibling(h2[:, : 3 * r], 1)
    g2 = ordered(h2[:, :r], h2_other[:, :r], 1)
    q2 = ordered(h2[:, r : 3 * r], h2_other[:, r : 3 * r], 1)
    tail = h2[:, 3 * r :]
    sums1 = tail + sibling(tail, 1)

    pair2 = lax.dynamic_index_in_dim(coupling2, gx >> 2, 0, keepdims=False)
    m2 = factor(g2, pair2)
    v2, h1 = level_update(1, m2, q2, sums1, ((gx >> 1) & 1).reshape(1))
    h1_other = sibling(h1, 2)
    g1 = ordered(h1[:, :r], h1_other[:, :r], 2)
    q1 = ordered(h1[:, r:], h1_other[:, r:], 2)
    m1 = factor(g1, coupling1[0])
    x = back(m1, q1, (gx >> 2).reshape(1), v3, v2)
    solved = apply_update(basis3, basis2, basis1, rhs, leaf_inverse, x)
    cores = []
    for level, m in ((3, m3), (2, m2), (1, m1)):
        count = 2**level * r // devices
        group = devices >> (level - 1)
        cores.append(core_rows(m, (place % group) * count, count))
    return (solved, *cores)


def solution(mesh):
    rows = P(("gx", "gy"), None)
    return jax.shard_map(
        per_device,
        mesh=mesh,
        in_specs=(rows, rows, rows, P(("gx", "gy")), rows, P(), P(), P()),
        out_specs=(rows, rows, rows, rows),
        check_vma=False,
    )
```

time: 857 us -> 374 us (0.44)
  other arithmetic: 391 us -> 13.4 us
  Pallas kernels: 0 us -> 111 us
  matrix products: 114 us -> 5.25 us
  local copies, waits for them, and re-layouts: 70.7 us -> 10.5 us
  starting transfers between devices: 36.8 us -> 7.48 us
  waiting for transfers between devices: 224 us -> 206 us
    another operation x51 -> x0, other arithmetic: 368 us -> none  [the longest x44 243 us: core_solve(): factor = jnp.linalg.cholesky(inner)]
    ppermute x18 -> x5, waiting for transfers between devices: 224 us -> 78.5 us  [sibling(): return lax.ppermute(value, 'gx', [(s, s ^ 1 << bit) for s in range(nx)])]
    psum x0 -> x1, waiting for transfers between devices: none -> 127 us  [per_device(): first = lax.psum(first, 'gy')]
    pallas_call x0 -> x8, Pallas kernels: none -> 111 us  [the longest x3 75.2 us: factor(): pl.pallas_call(factor_kernel, out_shape=jax.ShapeDtypeStruct((order, orde...]
    dot_general x24 -> x3, matrix products: 64 us -> 5.25 us  [core_rows(): lax.dot_general(own, m, (TN, ((), ())), precision=lax.Precision.HIGHEST,...]
    another operation x39 -> x0, matrix products: 49.6 us -> none  [the longest x21 28.7 us: core_solve(): lax.linalg.triangular_solve(factor, coupling_full.T, left_side=True, lowe...]
    another operation x52 -> x0, local copies, waits for them, and re-layouts: 43.5 us -> none  [the longest x40 41.5 us: core_solve(): lax.linalg.triangular_solve(factor, coupling_full.T, left_side=True, lowe...]
    ppermute x18 -> x5, starting transfers between devices: 36.8 us -> 7.44 us  [sibling(): return lax.ppermute(value, 'gx', [(s, s ^ 1 << bit) for s in range(nx)])]
  transfers between devices with their start and end apart: 18 -> 6, of which waited for: 18 -> 4; matrix products, arithmetic and copies ran while one was open for 1% -> 3% of each run, Pallas kernels for 0% -> 7%
where the time goes in v1:
time: 374 us; the launch traced here: 368 us
  waiting for transfers between devices  206 us (55%)
  Pallas kernels  111 us (30%)
  between operations  14.5 us (4%)
  other arithmetic  13.4 us (4%)
  local copies, waits for them, and re-layouts  10.5 us (3%)
  starting transfers between devices  7.48 us (2%)
  matrix products  5.25 us (1%)
    psum x1, waiting for transfers between devices, per_device(): first = lax.psum(first, 'gy')  127 us
    ppermute x5, waiting for transfers between devices, sibling(): return lax.ppermute(value, 'gx', [(s, s ^ 1 << bit) for s in range(nx)])  78.5 us
    pallas_call x3, Pallas kernels, factor(): pl.pallas_call(factor_kernel, out_shape=jax.ShapeDtypeStruct((order, orde...  75.2 us
    pallas_call x1, Pallas kernels, grams(): pl.pallas_call(gram_kernel, grid=(rows // tile,), in_specs=[block] * 4 +...  11.9 us
    pallas_call x2, Pallas kernels, level_update(): pl.pallas_call(lambda *refs: level_kernel(levels, *refs), out_shape=[jax....  11.2 us
    pallas_call x1, Pallas kernels, apply_update(): pl.pallas_call(apply_kernel, grid=(rows // tile,), in_specs=[block] * 4 +...  7.64 us
  transfers between devices with their start and end apart: 6, of which 4 were waited for; matrix products, arithmetic and copies ran while one was open for 3% of the time, Pallas kernels for 7%

profile of v1, /device:TPU:1, one launch (start us, length us, event | category | flops | bytes accessed | tf_op | source)
XLA Modules:
  0.0 367.5 jit_solution(15554475174703738290)
XLA Ops:
  7.2 0.0 copy-start
  7.2 0.0 all-reduce.3.cloned.1.call-start
  7.2 2.2 copy.13.leaf
  9.4 11.9 %grams.1 = (f32[256,256]{1,0:T(8,128)}, f32[256,2048]{1,0:T(8,128)}) custom-call(f32[2048,256]{1,0:T(8,128)} %b3.3, f32[2048,256]{1,0:T(8,128)} %b2.3, f32[2048,256]{1,0:T(8,128)} %b1.3, f32[2048,256]{1,0:T(8,128)} %rhs.3, f32[2048,1]{1,0:T(8,128)} %copy.13.leaf), custom_call_target="tpu_custom_call" | custom-call | tf_op jit(solution)/shard_map/grams/pallas_call | solution.py:64
  21.3 0.0 all-reduce.3.cloned.1.call-update
  21.4 127.2 %all-reduce.3.cloned.1.call-done = (f32[256,256]{1,0:T(8,128)}, f32[256,2048]{1,0:T(8,128)}) async-done(((f32[256,256]{1,0:T(8,128)}, f32[256,2048]{1,0:T(8,128)}), (f32[256,256]{1,0:T(8,128)}, f32[256,2048]{1,0:T(8,128)})) %all-reduce.3.cloned.1.call-update) | async-done | bytes 2359312 | tf_op jit(solution)/shard_map/psum | solution.py:270
  148.6 0.0 copy-start.6
  148.6 1.3 collective-permute-start.1
  149.9 0.3 collective-permute-start
  150.2 2.3 dynamic-slice_bitcast_fusion.1.coupling
  152.5 48.1 %collective-permute-done = f32[256,256]{1,0:T(8,128)S(1)} collective-permute-done((f32[256,256]{1,0:T(8,128)}, f32[256,256]{1,0:T(8,128)S(1)}, u32[]{:S(2)}, u32[]{:S(2)}) %collective-permute-start) | collective-permute-done | bytes 262176 | tf_op jit(solution)/shard_map/ppermute | solution.py:261
  200.5 0.0 copy-done.6
  200.6 0.8 pad_maximum_fusion.2.g
  201.4 25.1 %factor.3.refs_0_ = f32[512,512]{1,0:T(8,128)} custom-call(f32[512,256]{1,0:T(8,128)} %pad_maximum_fusion.2.g, f32[512,512]{1,0:T(8,128)} %dynamic-slice_bitcast_fusion.1.coupling), custom_call_target="tpu_custom_call" | custom-call | flops 2000000000 | bytes 3145728 | tf_op jit(solution)/shard_map/factor/pallas_call | solution.py:153
  226.5 0.0 collective-permute-done.1
  226.5 1.5 slice_select_fusion.1
  227.9 0.0 copy-start.4
  228.0 1.2 pad_maximum_fusion.refs_1_
  229.2 0.9 copy-done.4
  230.1 2.6 slice_add_fusion.refs_2_
  232.7 6.8 %level_update.2 = (f32[256,768]{1,0:T(8,128)}, f32[256,1280]{1,0:T(8,128)}) custom-call(f32[512,512]{1,0:T(8,128)} %factor.3.refs_0_, f32[512,768]{1,0:T(8,128)} %pad_maximum_fusion.refs_1_, f32[256,1280]{1,0:T(8,128)} %slice_add_fusion.refs_2_, s32[1]{0:T(128)} %bitcast.2.refs_3_), custom_call_target="tpu_custom_call" | custom-call | tf_op jit(solution)/shard_map/level_update/pallas_call | solution.py:188
  239.5 0.0 copy-start.1
  239.5 2.2 slice.47
  241.7 3.1 collective-permute-start.2
  244.7 1.9 slice.51
  246.6 0.1 collective-permute-start.3
  246.7 0.0 copy-done
  246.7 1.0 dynamic-slice_bitcast_fusion.coupling
  247.7 24.3 %collective-permute-done.3 = f32[256,512]{1,0:T(8,128)} collective-permute-done((f32[256,512]{1,0:T(8,128)}, f32[256,512]{1,0:T(8,128)}, u32[]{:S(2)}, u32[]{:S(2)}) %collective-permute-start.3) | collective-permute-done | bytes 524320 | tf_op jit(solution)/shard_map/ppermute | solution.py:261
  272.1 0.0 collective-permute-done.2
  272.1 0.0 copy-done.1
  272.1 2.2 slice_select_fusion.3
  274.3 1.0 pad_maximum_fusion.1.refs_1_
  275.3 1.0 slice_select_fusion.9
  276.3 0.8 pad_maximum_fusion.3.g
  277.1 25.1 %factor.4.refs_0_ = f32[512,512]{1,0:T(8,128)} custom-call(f32[512,256]{1,0:T(8,128)} %pad_maximum_fusion.3.g, f32[512,512]{1,0:T(8,128)} %dynamic-slice_bitcast_fusion.coupling), custom_call_target="tpu_custom_call" | custom-call | flops 2000000000 | bytes 3145728 | tf_op jit(solution)/shard_map/factor/pallas_call | solution.py:153
  302.2 0.0 copy-start.2
  302.2 4.4 %level_update.3 = (f32[256,512]{1,0:T(8,128)}, f32[256,512]{1,0:T(8,128)}) custom-call(f32[512,512]{1,0:T(8,128)} %factor.4.refs_0_, f32[512,512]{1,0:T(8,128)} %pad_maximum_fusion.1.refs_1_, f32[256,512]{1,0:T(8,128)} %get-tuple-element.24.refs_2_, s32[1]{0:T(128)} %bitcast.4.refs_3_), custom_call_target="tpu_custom_call" | custom-call | tf_op jit(solution)/shard_map/level_update/pallas_call | solution.py:188
  306.6 2.7 collective-permute-start.4
  309.3 0.0 copy-start.5
  309.3 2.7 fusion.4
  312.0 0.0 copy-done.2
  312.0 1.3 fusion.2
  313.3 6.1 %collective-permute-done.4 = f32[256,512]{1,0:T(8,128)} collective-permute-done((f32[256,512]{1,0:T(8,128)}, f32[256,512]{1,0:T(8,128)}, u32[]{:S(2)}, u32[]{:S(2)}) %collective-permute-start.4) | collective-permute-done | bytes 524320 | tf_op jit(solution)/shard_map/ppermute | solution.py:261
  319.4 0.0 copy-done.5
  319.4 1.1 slice_select_fusion.5
  320.5 1.1 pad_maximum_fusion.4
  321.6 25.1 %factor.5.m = f32[512,512]{1,0:T(8,128)} custom-call(f32[512,256]{1,0:T(8,128)} %get-tuple-element.31.g, f32[512,512]{1,0:T(8,128)} %bitcast.13), custom_call_target="tpu_custom_call" | custom-call | flops 2000000000 | bytes 3145728 | tf_op jit(solution)/shard_map/factor/pallas_call | solution.py:153
  346.7 4.6 %back.1.x = f32[768,256]{1,0:T(8,128)} custom-call(f32[512,512]{1,0:T(8,128)} %factor.5.m, f32[512,256]{1,0:T(8,128)} %get-tuple-element.32.q, s32[1]{0:T(128)} %bitcast.6.half, f32[256,768]{1,0:T(8,128)} %get-tuple-element.14.v3, f32[256,512]{1,0:T(8,128)} %get-tuple-element.15.v2), custom_call_target="tpu_custom_call" | custom-call | tf_op jit(solution)/shard_map/back/pallas_call | solution.py:212
  351.3 0.0 copy-start.3
  351.3 7.6 %apply_update.1 = f32[2048,256]{1,0:T(8,128)} custom-call(f32[2048,256]{1,0:T(8,128)} %b3.3, f32[2048,256]{1,0:T(8,128)} %b2.3, f32[2048,256]{1,0:T(8,128)} %b1.3, f32[2048,256]{1,0:T(8,128)} %rhs.3, f32[2048,1]{1,0:T(8,128)} %copy.13.leaf, f32[768,256]{1,0:T(8,128)} %back.1.x), custom_call_target="tpu_custom_call" | custom-call | tf_op jit(solution)/shard_map/apply_update/pallas_call | solution.py:234
  358.9 0.0 copy-done.3
  358.9 1.3 fusion
  (1 shorter events, 0.0 us)
Async XLA Ops:
  7.2 239.5 %copy-start = (f32[2,512,512]{2,1,0:T(8,128)S(1)}, f32[2,512,512]{2,1,0:T(8,128)}, u32[]{:S(2)}) copy-start(f32[2,512,512]{2,1,0:T(8,128)} %param.14) | copy-start | bytes 6291460
  7.2 141.4 %all-reduce.3.cloned.1.call-start = ((), (), s32[]{:S(2)}) async-start(), calls=%async_computation | async-start | bytes 4718592 | tf_op jit(solution)/shard_map/psum | solution.py:270
  148.6 51.9 %copy-start.6 = (f32[256,256]{1,0:T(8,128)S(1)}, f32[256,256]{1,0:T(8,128)}, u32[]{:S(2)}) copy-start(f32[256,256]{1,0:T(8,128)} %get-tuple-element.16) | copy-start | bytes 786436
  148.6 77.9 %collective-permute-start.1 = (f32[256,2048]{1,0:T(8,128)}, f32[256,2048]{1,0:T(8,128)}, u32[]{:S(2)}, u32[]{:S(2)}) collective-permute-start(f32[256,2048]{1,0:T(8,128)} %get-tuple-element.17), channel_id=1, source_target_pairs={{0,16},{16,0},{32,48},{48,32},{64,80},{80,64},{96,112},{112,96},{1... | collective-permute-start | bytes 6291464 | tf_op jit(solution)/shard_map/ppermute | solution.py:261
  149.9 50.7 %collective-permute-start = (f32[256,256]{1,0:T(8,128)}, f32[256,256]{1,0:T(8,128)S(1)}, u32[]{:S(2)}, u32[]{:S(2)}) collective-permute-start(f32[256,256]{1,0:T(8,128)} %get-tuple-element.16), channel_id=1, source_target_pairs={{0,16},{16,0},{32,48},{48,32},{64,80},{80,64},{96,112},{112,96},{1... | collective-permute-start | bytes 786440 | tf_op jit(solution)/shard_map/ppermute | solution.py:261
  227.9 2.2 copy-start.4
  239.5 32.6 %copy-start.1 = (f32[256,1280]{1,0:T(8,128)S(1)}, f32[256,1280]{1,0:T(8,128)}, u32[]{:S(2)}) copy-start(f32[256,1280]{1,0:T(8,128)} %get-tuple-element.12) | copy-start | bytes 3932164
  241.7 30.4 %collective-permute-start.2 = (f32[256,768]{1,0:T(8,128)}, f32[256,768]{1,0:T(8,128)}, u32[]{:S(2)}, u32[]{:S(2)}) collective-permute-start(f32[256,768]{1,0:T(8,128)} %slice.47), channel_id=1, source_target_pairs={{0,32},{16,48},{32,0},{48,16},{64,96},{80,112},{96,64},{112,80},{1... | collective-permute-start | bytes 2359304 | tf_op jit(solution)/shard_map/ppermute | solution.py:261
  246.6 25.5 %collective-permute-start.3 = (f32[256,512]{1,0:T(8,128)}, f32[256,512]{1,0:T(8,128)}, u32[]{:S(2)}, u32[]{:S(2)}) collective-permute-start(f32[256,512]{1,0:T(8,128)} %slice.51), channel_id=1, source_target_pairs={{0,32},{16,48},{32,0},{48,16},{64,96},{80,112},{96,64},{112,80},{1... | collective-permute-start | bytes 1572872 | tf_op jit(solution)/shard_map/ppermute | solution.py:261
  302.2 9.8 %copy-start.2 = (f32[512,512]{1,0:T(8,128)S(1)}, f32[512,512]{1,0:T(8,128)}, u32[]{:S(2)}) copy-start(f32[512,512]{1,0:T(8,128)} %factor.4.refs_0_) | copy-start | bytes 3145732
  306.6 12.7 %collective-permute-start.4 = (f32[256,512]{1,0:T(8,128)}, f32[256,512]{1,0:T(8,128)}, u32[]{:S(2)}, u32[]{:S(2)}) collective-permute-start(f32[256,512]{1,0:T(8,128)} %get-tuple-element.13), channel_id=1, source_target_pairs={{0,64},{16,80},{32,96},{48,112},{64,0},{80,16},{96,32},{112,48},{1... | collective-permute-start | bytes 1572872 | tf_op jit(solution)/shard_map/ppermute | solution.py:261
  309.3 10.1 %copy-start.5 = (f32[256,512]{1,0:T(8,128)S(1)}, f32[256,512]{1,0:T(8,128)}, u32[]{:S(2)}) copy-start(f32[256,512]{1,0:T(8,128)} %get-tuple-element.13) | copy-start | bytes 1572868
  351.3 7.6 %copy-start.3 = (f32[512,512]{1,0:T(8,128)S(1)}, f32[512,512]{1,0:T(8,128)}, u32[]{:S(2)}) copy-start(f32[512,512]{1,0:T(8,128)} %factor.5.m) | copy-start | bytes 3145732
Sparse Core Ops, SparseCore 0:
  21.5 127.0 all-reduce.2

commit v2 on v0

v2 whole, which is shorter than its diff:
```python
import jax
import jax.numpy as jnp
from jax import lax
from jax.experimental import pallas as pl
from jax.experimental.pallas import tpu as pltpu
from jax.sharding import PartitionSpec as P

F32 = jnp.float32
BF16 = jnp.bfloat16
NN = ((1,), (0,))
TN = ((0,), (0,))
W = 32
NB = 128
VMEM = pl.BlockSpec(memory_space=pltpu.VMEM)


def dot6(a, b, dims):
    return lax.dot_general(
        a, b, (dims, ((), ())), precision=lax.Precision.HIGHEST, preferred_element_type=F32
    )


def dot1(a, b, dims):
    return lax.dot_general(a, b, (dims, ((), ())), preferred_element_type=F32)


def split2(x):
    hi = x.astype(BF16)
    return hi, (x - hi.astype(F32)).astype(BF16)


def split3(x):
    hi = x.astype(BF16)
    rest = x - hi.astype(F32)
    mid = rest.astype(BF16)
    return hi, mid, (rest - mid.astype(F32)).astype(BF16)


def dot3(a, b, dims):
    (i,), (j,) = dims
    left = jnp.concatenate([a[0], a[0], a[1]], i)
    right = jnp.concatenate([b[0], b[1], b[0]], j)
    return dot1(left, right, dims)


MESH = pl.DeviceIdType.MESH


def where_am_i():
    gx = lax.axis_index("gx")
    gy = lax.axis_index("gy")
    core = gy % 2
    return gx, gy, core, gy // 2, gy + 1 - 2 * core, gx + 1 - 2 * (gx % 2)


def enter(peers):
    barrier = pltpu.get_barrier_semaphore()
    for peer in peers:
        pl.semaphore_signal(barrier, inc=1, device_id=peer, device_id_type=MESH)
    pl.semaphore_wait(barrier, len(peers))


def group_peers(chips):
    gx, gy, core, chip, other, sib = where_am_i()
    own = [(gx, 2 * ((chip + d) % chips) + core) for d in range(1, chips)]
    far = [(sib, 2 * ((chip + d) % chips) + core) for d in range(chips)]
    return [(gx, other)] + own + far


def remote(src, dst, send, recv, peer):
    return pltpu.make_async_remote_copy(
        src_ref=src, dst_ref=dst, send_sem=send, recv_sem=recv, device_id=peer, device_id_type=MESH
    )


def invert_factor(work):
    n = work.shape[0]
    lane = lax.broadcasted_iota(jnp.int32, (W, n), 1)
    sub = lax.broadcasted_iota(jnp.int32, (W, n), 0)
    for s in range(n // W):
        o = s * W
        block = work[o : o + W, :]
        cols = [
            jnp.stack(
                [
                    jnp.broadcast_to(block[8 * h :, o + k : o + k + 1], (W - 8 * h, n))
                    for k in range(8 * h, 8 * h + 8)
                ],
                0,
            )
            for h in range(W // 8)
        ]
        x = jnp.where((lane >= o) & (lane < o + W), jnp.where(lane - o == sub, 1.0, 0.0), block)
        for k in range(W):
            first = k // 8
            low = sub[8 * first :]
            column = cols[first][k % 8]
            d = column[k % 8 : k % 8 + 1]
            m = jnp.where(low > k, column * (1.0 / d), 0.0)
            for h in range(first, W // 8):
                from_h = 8 * (h - first)
                cols[h] = cols[h] - m[from_h:][None] * column[from_h : from_h + 8][:, None, :]
            tail = x[8 * first :]
            tail = tail - m * x[k : k + 1]
            tail = jnp.where(low == k, tail * lax.rsqrt(d), tail)
            x = tail if first == 0 else jnp.concatenate([x[: 8 * first], tail], 0)
        work[o : o + W, :] = jnp.where(lane < o + W, x, 0.0)
        t = o + W
        if t < n:
            v1, v2, v3 = split3(x)
            left = jnp.concatenate([v1, v1, v2, v1, v3, v2], 0)
            right = jnp.concatenate([v1, v2, v1, v3, v1, v2], 0)
            update = dot1(left, right, TN)
            below = lax.broadcasted_iota(jnp.int32, (n - t, n), 1)
            kept = jnp.where((below >= o) & (below < t), 0.0, work[t:, :])
            work[t:, :] = kept - update[t:, :]


GROUPS = (((0, 0),), ((0, 1), (1, 1)), ((0, 2), (1, 2), (2, 2)), ((0, 3), (1, 3), (2, 3)))
ORDER = {(1, 0): 0, (2, 0): 1, (2, 1): 3, (3, 0): 2, (3, 1): 4}
TILE = 256


def mega_kernel(
    chips, b3, b2, b1, rhs, leaf, cpl3, cpl2, cpl1, x, core3, core2, core1,
    raw, hi, lo, part, near, half, arrived, piece, far, pay, bag, g, q, s, h, q1, s1, tail, q2,
    coupling, c, work, m, p, v3, v2, krows,
    load_sem, near_sem, rs_sem, ag_sem, share_sem, far_sem, bag_sem, bshare_sem, ex_sem, exs_sem,
):
    gx, gy, core, chip, other, sib = where_am_i()
    rows, r = b3.shape
    order = 2 * r
    tiles = rows // TILE
    per = TILE // leaf.shape[1]
    hr = r // 2
    pr = hr // chips
    sides = (gx % 2, (gx // 2) % 2, (gx // 4) % 2)
    far_gx = (sib, gx + 2 - 4 * sides[1], gx + 4 - 8 * sides[2])
    side = sides[0]
    partner = (gx, other)

    loads = [
        pltpu.make_async_copy(b, raw.at[i], load_sem.at[i]) for i, b in enumerate((b3, b2, b1, rhs))
    ]
    loads += [
        pltpu.make_async_copy(src.at[at], coupling.at[i], load_sem.at[4 + i])
        for i, (src, at) in enumerate(((cpl3, gx // 2), (cpl2, gx // 4), (cpl1, 0)))
    ]
    for copy in loads:
        copy.start()
    peers = group_peers(chips)
    enter(peers + [(far_gx[1], gy), (far_gx[2], gy)])
    root = jnp.sqrt(leaf[...]).T

    nears = [
        remote(
            part.at[i, pl.ds(0, len(GROUPS[i])), pl.ds(pl.multiple_of((1 - core) * hr, hr), hr), :],
            near.at[i, pl.ds(0, len(GROUPS[i]))],
            near_sem.at[0, i], near_sem.at[1, i], partner,
        )
        for i in range(4)
    ]
    scatters = [
        [
            remote(
                half.at[
                    i, pl.ds(0, len(GROUPS[i])),
                    pl.ds(pl.multiple_of(((chip + d) % chips) * pr, pr), pr), :,
                ],
                arrived.at[i, d - 1, pl.ds(0, len(GROUPS[i]))],
                rs_sem.at[0, i, d - 1], rs_sem.at[1, i, d - 1], peers[d],
            )
            for d in range(1, chips)
        ]
        for i in range(4)
    ]
    row = pl.multiple_of(side * r + core * hr + chip * pr, pr)
    g_gather = [
        remote(
            piece.at[0, 0], g.at[0, pl.ds(row, pr), :], ag_sem.at[0, d], ag_sem.at[1, d], peer
        )
        for d, peer in enumerate(peers[1:])
    ]
    g_shares = []
    for t in range(2):
        at = g.at[0, pl.ds(pl.multiple_of(t * r + core * hr, hr), hr), :]
        g_shares.append(remote(at, at, share_sem.at[0, t], share_sem.at[1, t], partner))
    across = [
        remote(
            piece.at[i, pl.ds(1, len(GROUPS[i]) - 1)], far.at[i, pl.ds(0, len(GROUPS[i]) - 1)],
            far_sem.at[0, i], far_sem.at[1, i], (sib, gy),
        )
        for i in range(1, 4)
    ]
    bag_rows = [pr + (pr // 2) * (len(GROUPS[i]) - 1) for i in range(1, 4)]
    gathers = [
        [
            remote(
                pay.at[i, pl.ds(0, n), :], bag.at[i, side, core, chip, pl.ds(0, n), :],
                bag_sem.at[0, i, d], bag_sem.at[1, i, d], peer,
            )
            for d, peer in enumerate(peers[1:])
        ]
        for i, n in enumerate(bag_rows)
    ]
    bag_shares = [
        [
            remote(
                bag.at[i, t, core, :, pl.ds(0, n), :], bag.at[i, t, core, :, pl.ds(0, n), :],
                bshare_sem.at[0, i, t], bshare_sem.at[1, i, t], partner,
            )
            for t in range(2)
        ]
        for i, n in enumerate(bag_rows)
    ]

    def local(i):
        loads[i].wait()
        for t in range(tiles):
            scale = jnp.concatenate([root[:, t * per + u : t * per + u + 1] for u in range(per)], 0)
            upper, lower = split2(raw[i, t * TILE : (t + 1) * TILE, :] * scale)
            hi[i, t * TILE : (t + 1) * TILE, :] = upper
            lo[i, t * TILE : (t + 1) * TILE, :] = lower
        for n in range(len(GROUPS[i])):
            part[i, n] = jnp.zeros((r, r), F32)

        def tile(t, carry):
            at = pl.ds(pl.multiple_of(t * TILE, TILE), TILE)
            for n, (a, b) in enumerate(GROUPS[i]):
                part[i, n] += dot3((hi[a, at, :], lo[a, at, :]), (hi[b, at, :], lo[b, at, :]), TN)
            return carry

        lax.fori_loop(0, tiles, tile, 0)
        nears[i].start()

    def scatter(i):
        n = len(GROUPS[i])
        nears[i].wait_recv()
        half[i, 0:n] = part[i, 0:n, pl.ds(pl.multiple_of(core * hr, hr), hr), :] + near[i, 0:n]
        for copy in scatters[i]:
            copy.start()

    def collect(i):
        n = len(GROUPS[i])
        total = half[i, 0:n, pl.ds(pl.multiple_of(chip * pr, pr), pr), :]
        for d, copy in enumerate(scatters[i]):
            copy.wait_recv()
            total = total + arrived[i, d, 0:n]
        piece[i, 0:n] = total
        if i > 0:
            across[i - 1].start()

    def gather(i):
        across[i - 1].wait_recv()
        pay[i - 1, 0:pr, :] = piece[i, 0]
        keep = pl.ds(pl.multiple_of(side * (pr // 2), pr // 2), pr // 2)
        for n in range(len(GROUPS[i]) - 1):
            at = pr + n * (pr // 2)
            pay[i - 1, at : at + pr // 2, :] = piece[i, n + 1, keep, :] + far[i, n, keep, :]
        for copy in gathers[i - 1]:
            copy.start()
        bag[i - 1, side, core, chip, 0 : bag_rows[i - 1], :] = pay[i - 1, 0 : bag_rows[i - 1], :]

    def share(i):
        for copy in gathers[i - 1]:
            copy.wait_recv()
        for copy in bag_shares[i - 1]:
            copy.start()

    def unpack(i):
        for copy in bag_shares[i - 1]:
            copy.wait_recv()
        q[:, (i - 1) * r : i * r] = bag[i - 1, :, :, :, 0:pr, :].reshape(order, r)
        for n in range(len(GROUPS[i]) - 1):
            at = pr + n * (pr // 2)
            for t in range(2):
                s[ORDER[i, n], :, t] = bag[i - 1, t, :, :, at : at + pr // 2, :].reshape(
                    2 * chips, pr // 2, r
                )

    def swap(level, src, dst, n):
        return remote(src, dst, ex_sem.at[0, level, n], ex_sem.at[1, level, n], (far_gx[level], gy))

    def pass_on(level, ref, n):
        return remote(ref, ref, exs_sem.at[0, level, n], exs_sem.at[1, level, n], partner)

    mine = pl.ds(pl.multiple_of(core * hr, hr), hr)
    ex_g, ex_q, sh_g, sh_q = {}, {}, {}, {}
    for level, qs in ((1, q1), (2, q2)):
        to = pl.ds(pl.multiple_of(sides[level] * r + core * hr, hr), hr)
        come = pl.ds(pl.multiple_of((1 - sides[level]) * r + core * hr, hr), hr)
        ex_g[level] = swap(level, h.at[level - 1, 0, mine, :], g.at[level, to, :], 0)
        ex_q[level] = swap(level, qs.at[to, :], qs.at[to, :], 1)
        sh_g[level] = pass_on(level, g.at[level, come, :], 0)
        sh_q[level] = pass_on(level, qs.at[come, :], 1)
    ex_s = swap(1, s1.at[mine, :], tail, 2)
    sh_s = pass_on(1, s1.at[mine, :], 2)

    local(0)
    local(1)
    scatter(0)
    local(2)
    collect(0)
    g[0, pl.ds(row, pr), :] = piece[0, 0]
    for copy in g_gather:
        copy.start()
    scatter(1)
    local(3)
    scatter(2)
    collect(1)
    for copy in g_gather:
        copy.wait_recv()
    for copy in g_shares:
        copy.start()
    scatter(3)
    gather(1)
    collect(2)
    for copy in g_shares:
        copy.wait_recv()
    for copy in loads[4:]:
        copy.wait()

    eye = jnp.where(
        lax.broadcasted_iota(jnp.int32, (NB, NB), 0) == lax.broadcasted_iota(jnp.int32, (NB, NB), 1),
        1.0,
        0.0,
    )
    steps = order // NB

    def receive_q(level):
        ex_q[level].wait_recv()
        sh_q[level].start()

    def hook(level, j):
        if (level, j) == (0, 0):
            gather(2)
            collect(3)
        elif (level, j) == (0, 1):
            gather(3)
            share(1)
        elif (level, j) == (0, 2):
            share(2)
        elif (level, j) == (0, 3):
            share(3)
            unpack(1)
        elif (level, j) == (1, 2):
            receive_q(1)
            ex_s.wait()
            s1[mine, :] = s1[mine, :] + tail[...]
            sh_s.start()
        elif (level, j) == (2, 1):
            receive_q(2)

    def core_block(out, level, count):
        place = gx * 2 * chips + gy
        start = (place % (4 * chips << level)) * count
        at = pl.ds(pl.multiple_of((start // NB) * NB, NB), NB)
        krows[...] = dot3(split2(m[:, at]), split2(m[...]), TN)
        inner = start % NB
        if count % 8 == 0:
            out[...] = krows[pl.ds(pl.multiple_of(inner, 8), count), :]
        else:
            eight = krows[pl.ds(pl.multiple_of((inner // 8) * 8, 8), 8), :]
            out[...] = jnp.where(inner % 8 == 0, eight[:count], eight[count:])

    def own_of(level):
        return split2(m[:, pl.ds(pl.multiple_of(sides[level] * r, r), r)])

    def column(i):
        return split2(p[:, i * r : (i + 1) * r])

    def after(level):
        ms = split2(m[...])
        if level == 0:
            p[:, 0:r] = dot3(ms, split2(q[:, 0:r]), NN)
            p2 = column(0)
            h[0, 0] = s[0].reshape(r, r) - dot3(p2, p2, TN)
            ex_g[1].start()
            g[1, pl.ds(pl.multiple_of(sides[1] * r, r), r), :] = h[0, 0]
            unpack(2)
            unpack(3)
            p[:, r:] = dot3(ms, split2(q[:, r:]), NN)
            p1, pc = column(1), column(2)
            at = pl.ds(pl.multiple_of(sides[1] * r, r), r)
            q1[at, 0:r] = s[1].reshape(r, r) - dot3(p2, p1, TN)
            q1[at, r:] = s[2].reshape(r, r) - dot3(p2, pc, TN)
            ex_q[1].start()
            s1[:, 0:r] = s[3].reshape(r, r) - dot3(p1, p1, TN)
            s1[:, r:] = s[4].reshape(r, r) - dot3(p1, pc, TN)
            ex_s.start()
            ex_g[1].wait_recv()
            sh_g[1].start()
            v3[...] = dot3(own_of(0), split2(p[...]), TN)
            core_block(core3, 0, 16)
            sh_g[1].wait_recv()
        elif level == 1:
            sh_q[1].wait_recv()
            sh_s.wait_recv()
            p[:, 0:r] = dot3(ms, split2(q1[:, 0:r]), NN)
            p1 = column(0)
            h[1, 0] = s1[:, 0:r] - dot3(p1, p1, TN)
            ex_g[2].start()
            g[2, pl.ds(pl.multiple_of(sides[2] * r, r), r), :] = h[1, 0]
            p[:, r : 2 * r] = dot3(ms, split2(q1[:, r:]), NN)
            q2[pl.ds(pl.multiple_of(sides[2] * r, r), r), :] = s1[:, r:] - dot3(p1, column(1), TN)
            ex_q[2].start()
            ex_g[2].wait_recv()
            sh_g[2].start()
            v2[...] = dot3(own_of(1), split2(p[:, 0 : 2 * r]), TN)
            core_block(core2, 1, 8)
            sh_g[2].wait_recv()
        else:
            sh_q[2].wait_recv()
            x1 = dot3(own_of(2), split2(dot3(ms, split2(q2[...]), NN)), TN)
            t1 = split2(x1)
            x2 = v2[:, r:] - dot3(split2(v2[:, :r]), t1, NN)
            t2 = split2(x2)
            x3 = v3[:, 2 * r :] - dot3(split2(v3[:, :r]), t2, NN)
            x3 = x3 - dot3(split2(v3[:, r : 2 * r]), t1, NN)
            x[0:r, :] = x3
            x[r : 2 * r, :] = x2
            x[2 * r :, :] = x1
            core_block(core1, 2, 4)

    def one_level(level, carry):
        full = coupling[level]
        gl = jnp.concatenate(
            [dot6(g[level, :r, :], full[:r, :], NN), dot6(g[level, r:, :], full[r:, :], NN)], 0
        )
        for j in range(steps):
            o = j * NB
            c[o : o + NB, o:order] = dot6(full[:, o : o + NB], gl[:, o:], TN)
            c[o : o + NB, order:] = full[:, o : o + NB].T

        def step(j, carry):
            for jj in range(steps):

                @pl.when(j == jj)
                def _(o=jj * NB):
                    work[...] = c[o : o + NB, o : o + NB] + eye

            invert_factor(work)
            for jj in range(steps):

                @pl.when(j == jj)
                def _(jj=jj, o=jj * NB, t=jj * NB + NB):
                    out = dot6(work[...], c[o : o + NB, t:], NN)
                    m[o : o + NB, :] = out[:, order - t :]
                    for w in range(t, order, NB):
                        c[w : w + NB, w:] = c[w : w + NB, w:] - dot6(
                            out[:, w - t : w - t + NB], out[:, w - t :], TN
                        )

            for lv, jj in ((0, 0), (0, 1), (0, 2), (0, 3), (1, 2), (2, 1)):

                @pl.when((level == lv) & (j == jj))
                def _(lv=lv, jj=jj):
                    hook(lv, jj)

            return carry

        lax.fori_loop(0, steps, step, 0)
        for lv in range(3):

            @pl.when(level == lv)
            def _(lv=lv):
                after(lv)

        return carry

    lax.fori_loop(0, 3, one_level, 0)
    sends = [*nears, *g_gather, *g_shares, *across, ex_g[1], ex_g[2], ex_q[1], ex_q[2]]
    sends += [sh_g[1], sh_g[2], sh_q[1], sh_q[2], sh_s]
    for copies in (*scatters, *gathers, *bag_shares):
        sends += copies
    for copy in sends:
        copy.wait_send()


def mega(b3, b2, b1, rhs, leaf, cpl3, cpl2, cpl1):
    rows, r = b3.shape
    order = 2 * r
    chips = lax.axis_size("gy") // 2
    hr = r // 2
    pr = hr // chips
    most = max(len(y) for y in GROUPS)
    wide = pr + (pr // 2) * (most - 1)
    hbm = pl.BlockSpec(memory_space=pl.ANY)
    dma = pltpu.SemaphoreType.DMA

    def vmem(*shape):
        return pltpu.VMEM(shape, F32)

    return pl.pallas_call(
        lambda *refs: mega_kernel(chips, *refs),
        in_specs=[hbm] * 4 + [VMEM] + [hbm] * 3,
        out_specs=[VMEM] * 4,
        out_shape=[
            jax.ShapeDtypeStruct(shape, F32)
            for shape in ((3 * r, r), (16, order), (8, order), (4, order))
        ],
        scratch_shapes=[
            vmem(4, rows, r),
            pltpu.VMEM((4, rows, r), BF16),
            pltpu.VMEM((4, rows, r), BF16),
            vmem(4, most, r, r),
            vmem(4, most, hr, r),
            vmem(4, most, hr, r),
            vmem(4, chips - 1, most, pr, r),
            vmem(4, most, pr, r),
            vmem(4, most - 1, pr, r),
            vmem(3, wide, r),
            vmem(3, 2, 2, chips, wide, r),
            vmem(3, order, r),
            vmem(order, 3 * r),
            vmem(5, 2 * chips, 2, pr // 2, r),
            vmem(2, 1, r, r),
            vmem(order, 2 * r),
            vmem(r, 2 * r),
            vmem(hr, 2 * r),
            vmem(order, r),
            vmem(3, order, order),
            vmem(order, 2 * order),
            vmem(NB, NB),
            vmem(order, order),
            vmem(order, 3 * r),
            vmem(r, 3 * r),
            vmem(r, 2 * r),
            vmem(NB, order),
            dma((7,)),
            dma((2, 4)),
            dma((2, 4, chips - 1)),
            dma((2, 2 * chips - 1)),
            dma((2, 2)),
            dma((2, 4)),
            dma((2, 3, 2 * chips - 1)),
            dma((2, 3, 2)),
            dma((2, 3, 3)),
            dma((2, 3, 3)),
        ],
        compiler_params=pltpu.CompilerParams(
            collective_id=0, has_side_effects=True, vmem_limit_bytes=56 << 20
        ),
        name="mega",
    )(b3, b2, b1, rhs, leaf.reshape(rows // 128, 128), cpl3, cpl2, cpl1)


def apply_kernel(b3, b2, b1, rhs, leaf, x, k3, k2, k1, out, core3, core2, core1):
    r = b3.shape[1]

    @pl.when(pl.program_id(0) == 0)
    def _():
        core3[...] = k3[...]
        core2[...] = k2[...]
        core1[...] = k1[...]

    xs = split2(x[...])
    total = rhs[...]
    for i, b in enumerate((b3, b2, b1)):
        total = total - dot3(split2(b[...]), tuple(y[i * r : (i + 1) * r] for y in xs), NN)
    turned = leaf[0].T
    out[...] = total * jnp.concatenate([turned[:, u : u + 1] for u in range(leaf.shape[1])], 0)


def apply_update(b3, b2, b1, rhs, leaf, x, cores):
    rows, r = b3.shape
    tile = 512
    block = pl.BlockSpec((tile, r), lambda i: (i, 0))
    whole = [pl.BlockSpec(k.shape, lambda i: (0, 0)) for k in cores]
    return pl.pallas_call(
        apply_kernel,
        grid=(rows // tile,),
        in_specs=[block] * 4
        + [
            pl.BlockSpec((1, tile // 128, 128), lambda i: (i, 0, 0)),
            pl.BlockSpec(x.shape, lambda i: (0, 0)),
        ]
        + whole,
        out_specs=[block] + whole,
        out_shape=[jax.ShapeDtypeStruct(rhs.shape, F32)]
        + [jax.ShapeDtypeStruct(k.shape, F32) for k in cores],
        name="apply_update",
    )(b3, b2, b1, rhs, leaf.reshape(rows // tile, tile // 128, 128), x, *cores)


def per_device(basis3, basis2, basis1, leaf_inverse, rhs, coupling3, coupling2, coupling1):
    x, *cores = mega(
        basis3, basis2, basis1, rhs, leaf_inverse, coupling3, coupling2, coupling1
    )
    return tuple(apply_update(basis3, basis2, basis1, rhs, leaf_inverse, x, cores))


def solution(mesh):
    rows = P(("gx", "gy"), None)
    return jax.shard_map(
        per_device,
        mesh=mesh,
        in_specs=(rows, rows, rows, P(("gx", "gy")), rows, P(), P(), P()),
        out_specs=(rows, rows, rows, rows),
        check_vma=False,
    )
```

time: 857 us -> 124 us (0.14); the launches traced: 845 us -> 123 us
  other arithmetic: 391 us -> 0 us
  waiting for transfers between devices: 224 us -> 0 us
  Pallas kernels: 0 us -> 122 us
  matrix products: 114 us -> 0 us
  local copies, waits for them, and re-layouts: 70.7 us -> 0 us
  starting transfers between devices: 36.8 us -> 0 us
  between operations: 9.51 us -> 0.64 us
    another operation x51 -> x0, other arithmetic: 368 us -> none  [the longest x44 243 us: core_solve(): factor = jnp.linalg.cholesky(inner)]
    ppermute x18 -> x0, waiting for transfers between devices: 224 us -> none  [swapped(): return lax.ppermute(value, axis, pairs)]
    pallas_call x0 -> x2, Pallas kernels: none -> 122 us  [the longest x1 115 us: mega(): pl.pallas_call(lambda *refs: mega_kernel(chips, *refs), in_specs=[hbm] *...]
    dot_general x24 -> x0, matrix products: 64 us -> none  [the longest x3 23.7 us: per_device(): jnp.einsum('nr,nw->rw', basis_now, solved, precision=highest_precision)]
    another operation x39 -> x0, matrix products: 49.6 us -> none  [the longest x21 28.7 us: core_solve(): lax.linalg.triangular_solve(factor, coupling_full.T, left_side=True, lowe...]
    another operation x52 -> x0, local copies, waits for them, and re-layouts: 43.5 us -> none  [the longest x40 41.5 us: core_solve(): lax.linalg.triangular_solve(factor, coupling_full.T, left_side=True, lowe...]
    ppermute x18 -> x0, starting transfers between devices: 36.8 us -> none  [swapped(): return lax.ppermute(value, axis, pairs)]
  transfers between devices with their start and end apart: 18 -> 0, of which waited for: 18 -> 0; matrix products, arithmetic and copies ran while one was open for 1% -> 0% of each run, Pallas kernels for 0% -> 0%
where the time goes in v2:
time: 124 us; the launch traced here: 123 us
  Pallas kernels  122 us (98%)
    pallas_call x1, Pallas kernels, mega(): pl.pallas_call(lambda *refs: mega_kernel(chips, *refs), in_specs=[hbm] *...  115 us
    pallas_call x1, Pallas kernels, apply_update(): pl.pallas_call(apply_kernel, grid=(rows // tile,), in_specs=[block] * 4 +...  7.28 us

profile of v2, /device:TPU:1, one launch (start us, length us, event | category | flops | bytes accessed | tf_op | source)
XLA Modules:
  0.0 122.8 jit_solution(15426360159909511171)
XLA Ops:
  0.6 114.8 %mega.1 = (f32[768,256]{1,0:T(8,128)}, f32[16,512]{1,0:T(8,128)}, f32[8,512]{1,0:T(8,128)}, f32[4,512]{1,0:T(4,128)}) custom-call(f32[2048,256]{1,0:T(8,128)} %b3.1, f32[2048,256]{1,0:T(8,128)} %b2.1, f32[2048,256]{1,0:T(8,128)} %b1.1, f32[2048,256]{1,0:T(8,128)} %rhs.1, f32[16,128]{1,0:T(8,128)} %bitcast.2, f32[4,512,512]{2,1,0:T(8,128)} %refs_5_.1, ...), custom_call_target="tpu_custom_call" | custom-call | tf_op jit(solution)/shard_map/mega/pallas_call | solution.py:494
  115.5 7.3 %apply_update.1 = (f32[2048,256]{1,0:T(8,128)}, f32[16,512]{1,0:T(8,128)}, f32[8,512]{1,0:T(8,128)}, f32[4,512]{1,0:T(4,128)}) custom-call(f32[2048,256]{1,0:T(8,128)} %b3.1, f32[2048,256]{1,0:T(8,128)} %b2.1, f32[2048,256]{1,0:T(8,128)} %b1.1, f32[2048,256]{1,0:T(8,128)} %rhs.1, f32[4,4,128]{2,1,0:T(4,128)} %bitcast.3, f32[768,256]{1,0:T(8,128)} %get-tuple-element.8.x, ...), custom_call_target="tpu_custom_call" | custom-call | tf_op jit(solution)/shard_map/apply_update/pallas_call | solution.py:570

commit v3 on v2

--- a/solution.py
+++ b/solution.py
@@ -15,9 +15,10 @@
 
 
 def dot6(a, b, dims):
-    return lax.dot_general(
-        a, b, (dims, ((), ())), precision=lax.Precision.HIGHEST, preferred_element_type=F32
-    )
+    (i,), (j,) = dims
+    left = jnp.concatenate([a[0], a[0], a[1], a[0], a[2], a[1]], i)
+    right = jnp.concatenate([b[0], b[1], b[0], b[2], b[0], b[1]], j)
+    return dot1(left, right, dims)
 
 
 def dot1(a, b, dims):
@@ -53,11 +54,14 @@
     return gx, gy, core, gy // 2, gy + 1 - 2 * core, gx + 1 - 2 * (gx % 2)
 
 
-def enter(peers):
+def greet(peers):
     barrier = pltpu.get_barrier_semaphore()
     for peer in peers:
         pl.semaphore_signal(barrier, inc=1, device_id=peer, device_id_type=MESH)
-    pl.semaphore_wait(barrier, len(peers))
+
+
+def all_met(peers):
+    pl.semaphore_wait(pltpu.get_barrier_semaphore(), len(peers))
 
 
 def group_peers(chips):
@@ -73,44 +77,43 @@
     )
 
 
-def invert_factor(work):
+def invert_factor(work, spread):
     n = work.shape[0]
-    lane = lax.broadcasted_iota(jnp.int32, (W, n), 1)
-    sub = lax.broadcasted_iota(jnp.int32, (W, n), 0)
+    parts = W // 8
+    lane = lax.broadcasted_iota(jnp.int32, (8, n), 1)
+    sub = lax.broadcasted_iota(jnp.int32, (8, n), 0)
+    wide = lax.broadcasted_iota(jnp.int32, (W, n), 1)
     for s in range(n // W):
         o = s * W
-        block = work[o : o + W, :]
-        cols = [
-            jnp.stack(
-                [
-                    jnp.broadcast_to(block[8 * h :, o + k : o + k + 1], (W - 8 * h, n))
-                    for k in range(8 * h, 8 * h + 8)
-                ],
-                0,
-            )
-            for h in range(W // 8)
+        block = [work[o + 8 * h : o + 8 * h + 8, :] for h in range(parts)]
+        for k in range(W):
+            for h in range(k // 8, parts):
+                spread[k, h] = jnp.broadcast_to(block[h][:, o + k : o + k + 1], (8, n))
+        col = {(k, h): spread[k, h] for k in range(W) for h in range(k // 8, parts)}
+        inside = (lane >= o) & (lane < o + W)
+        x = [
+            jnp.where(inside, jnp.where(lane - o == sub + 8 * h, 1.0, 0.0), block[h])
+            for h in range(parts)
         ]
-        x = jnp.where((lane >= o) & (lane < o + W), jnp.where(lane - o == sub, 1.0, 0.0), block)
         for k in range(W):
-            first = k // 8
-            low = sub[8 * first :]
-            column = cols[first][k % 8]
-            d = column[k % 8 : k % 8 + 1]
-            m = jnp.where(low > k, column * (1.0 / d), 0.0)
-            for h in range(first, W // 8):
-                from_h = 8 * (h - first)
-                cols[h] = cols[h] - m[from_h:][None] * column[from_h : from_h + 8][:, None, :]
-            tail = x[8 * first :]
-            tail = tail - m * x[k : k + 1]
-            tail = jnp.where(low == k, tail * lax.rsqrt(d), tail)
-            x = tail if first == 0 else jnp.concatenate([x[: 8 * first], tail], 0)
-        work[o : o + W, :] = jnp.where(lane < o + W, x, 0.0)
+            g, e = k // 8, k % 8
+            d = col[k, g][e : e + 1]
+            recip = 1.0 / d
+            pivot_row = x[g][e : e + 1]
+            for h in range(g, parts):
+                m = col[k, h] * recip
+                if h == g:
+                    m = jnp.where(sub > e, m, 0.0)
+                for j in range(k + 1, min(W, 8 * h + 8)):
+                    col[j, h] = col[j, h] - m * col[k, j // 8][j % 8 : j % 8 + 1]
+                x[h] = x[h] - m * pivot_row
+            x[g] = jnp.where(sub == e, x[g] * lax.rsqrt(d), x[g])
+        v = jnp.concatenate(x, 0)
+        work[o : o + W, :] = jnp.where(wide < o + W, v, 0.0)
         t = o + W
         if t < n:
-            v1, v2, v3 = split3(x)
-            left = jnp.concatenate([v1, v1, v2, v1, v3, v2], 0)
-            right = jnp.concatenate([v1, v2, v1, v3, v1, v2], 0)
-            update = dot1(left, right, TN)
+            v3 = split3(v)
+            update = dot6(v3, v3, TN)
             below = lax.broadcasted_iota(jnp.int32, (n - t, n), 1)
             kept = jnp.where((below >= o) & (below < t), 0.0, work[t:, :])
             work[t:, :] = kept - update[t:, :]
@@ -118,13 +121,13 @@
 
 GROUPS = (((0, 0),), ((0, 1), (1, 1)), ((0, 2), (1, 2), (2, 2)), ((0, 3), (1, 3), (2, 3)))
 ORDER = {(1, 0): 0, (2, 0): 1, (2, 1): 3, (3, 0): 2, (3, 1): 4}
-TILE = 256
+TILE = 512
 
 
 def mega_kernel(
     chips, b3, b2, b1, rhs, leaf, cpl3, cpl2, cpl1, x, core3, core2, core1,
-    raw, hi, lo, part, near, half, arrived, piece, far, pay, bag, g, q, s, h, q1, s1, tail, q2,
-    coupling, c, work, m, p, v3, v2, krows,
+    raw, hi_t, lo_t, part, near, half, arrived, piece, far, pay, bag, g, q, s, h, q1, s1, tail, q2,
+    coupling, turned, l_parts, lt_parts, c, work, spread, m, p, v3, v2, krows,
     load_sem, near_sem, rs_sem, ag_sem, share_sem, far_sem, bag_sem, bshare_sem, ex_sem, exs_sem,
 ):
     gx, gy, core, chip, other, sib = where_am_i()
@@ -146,10 +149,12 @@
         pltpu.make_async_copy(src.at[at], coupling.at[i], load_sem.at[4 + i])
         for i, (src, at) in enumerate(((cpl3, gx // 2), (cpl2, gx // 4), (cpl1, 0)))
     ]
-    for copy in loads:
+    loads[0].start()
+    peers = group_peers(chips)
+    everyone = peers + [(far_gx[1], gy), (far_gx[2], gy)]
+    greet(everyone)
+    for copy in loads[1:]:
         copy.start()
-    peers = group_peers(chips)
-    enter(peers + [(far_gx[1], gy), (far_gx[2], gy)])
     root = jnp.sqrt(leaf[...]).T
 
     nears = [
@@ -216,21 +221,21 @@
 
     def local(i):
         loads[i].wait()
+        n = len(GROUPS[i])
         for t in range(tiles):
+            at = slice(t * TILE, (t + 1) * TILE)
             scale = jnp.concatenate([root[:, t * per + u : t * per + u + 1] for u in range(per)], 0)
-            upper, lower = split2(raw[i, t * TILE : (t + 1) * TILE, :] * scale)
-            hi[i, t * TILE : (t + 1) * TILE, :] = upper
-            lo[i, t * TILE : (t + 1) * TILE, :] = lower
-        for n in range(len(GROUPS[i])):
-            part[i, n] = jnp.zeros((r, r), F32)
-
-        def tile(t, carry):
-            at = pl.ds(pl.multiple_of(t * TILE, TILE), TILE)
-            for n, (a, b) in enumerate(GROUPS[i]):
-                part[i, n] += dot3((hi[a, at, :], lo[a, at, :]), (hi[b, at, :], lo[b, at, :]), TN)
-            return carry
-
-        lax.fori_loop(0, tiles, tile, 0)
+            upper, lower = split2(raw[i, at, :] * scale)
+            if i < 3:
+                hi_t[i, :, at] = upper.T
+                lo_t[i, :, at] = lower.T
+            left = tuple(
+                jnp.concatenate([z[a, :, at] for a, b in GROUPS[i]], 0) for z in (hi_t, lo_t)
+            )
+            sums = dot3(left, (upper, lower), NN).reshape(n, r, r)
+            part[i, 0:n] = sums if t == 0 else part[i, 0:n] + sums
+        if i == 0:
+            all_met(everyone)
         nears[i].start()
 
     def scatter(i):
@@ -295,6 +300,14 @@
         sh_q[level] = pass_on(level, qs.at[come, :], 1)
     ex_s = swap(1, s1.at[mine, :], tail, 2)
     sh_s = pass_on(1, s1.at[mine, :], 2)
+
+    def prepare(level):
+        loads[4 + level].wait()
+        across_rows = coupling[level].T
+        turned[level] = across_rows
+        for n, (y, z) in enumerate(zip(split3(coupling[level]), split3(across_rows))):
+            l_parts[level, n] = y
+            lt_parts[level, n] = z
 
     local(0)
     local(1)
@@ -315,10 +328,9 @@
     scatter(3)
     gather(1)
     collect(2)
+    prepare(0)
     for copy in g_shares:
         copy.wait_recv()
-    for copy in loads[4:]:
-        copy.wait()
 
     eye = jnp.where(
         lax.broadcasted_iota(jnp.int32, (NB, NB), 0) == lax.broadcasted_iota(jnp.int32, (NB, NB), 1),
@@ -388,6 +400,7 @@
             s1[:, 0:r] = s[3].reshape(r, r) - dot3(p1, p1, TN)
             s1[:, r:] = s[4].reshape(r, r) - dot3(p1, pc, TN)
             ex_s.start()
+            prepare(1)
             ex_g[1].wait_recv()
             sh_g[1].start()
             v3[...] = dot3(own_of(0), split2(p[...]), TN)
@@ -404,6 +417,7 @@
             p[:, r : 2 * r] = dot3(ms, split2(q1[:, r:]), NN)
             q2[pl.ds(pl.multiple_of(sides[2] * r, r), r), :] = s1[:, r:] - dot3(p1, column(1), TN)
             ex_q[2].start()
+            prepare(2)
             ex_g[2].wait_recv()
             sh_g[2].start()
             v2[...] = dot3(own_of(1), split2(p[:, 0 : 2 * r]), TN)
@@ -423,43 +437,55 @@
             core_block(core1, 2, 4)
 
     def one_level(level, carry):
-        full = coupling[level]
+        l3 = [l_parts[level, n] for n in range(3)]
+        lt3 = [lt_parts[level, n] for n in range(3)]
+        g3 = split3(g[level])
         gl = jnp.concatenate(
-            [dot6(g[level, :r, :], full[:r, :], NN), dot6(g[level, r:, :], full[r:, :], NN)], 0
+            [
+                dot6([y[at] for y in g3], [y[at] for y in l3], NN)
+                for at in (slice(0, r), slice(r, order))
+            ],
+            0,
         )
+        gl3 = split3(gl)
+        for o in range(0, order, NB):
+            at = slice(o, o + NB)
+            c[at, o:order] = dot6([y[at] for y in lt3], [y[:, o:] for y in gl3], NN)
+            c[at, order:] = turned[level, at, :]
+        work[...] = c[0:NB, 0:NB] + eye
+        behind = None
         for j in range(steps):
             o = j * NB
-            c[o : o + NB, o:order] = dot6(full[:, o : o + NB], gl[:, o:], TN)
-            c[o : o + NB, order:] = full[:, o : o + NB].T
-
-        def step(j, carry):
-            for jj in range(steps):
-
-                @pl.when(j == jj)
-                def _(o=jj * NB):
-                    work[...] = c[o : o + NB, o : o + NB] + eye
-
-            invert_factor(work)
-            for jj in range(steps):
-
-                @pl.when(j == jj)
-                def _(jj=jj, o=jj * NB, t=jj * NB + NB):
-                    out = dot6(work[...], c[o : o + NB, t:], NN)
-                    m[o : o + NB, :] = out[:, order - t :]
-                    for w in range(t, order, NB):
+            t = o + NB
+            u = t + NB
+            if behind is not None:
+                behind()
+            invert_factor(work, spread)
+            inverse = split3(work[...])
+            if t < order:
+                near_row = split3(dot6(inverse, split3(c[o:t, t:u]), NN))
+                work[...] = c[t:u, t:u] - dot6(near_row, near_row, TN) + eye
+
+                def behind(o=o, t=t, u=u, inverse=inverse, near_row=near_row):
+                    out = dot6(inverse, split3(c[o:t, u:]), NN)
+                    m[o:t, :] = out[:, order - u :]
+                    out3 = split3(out)
+                    c[t:u, u:] = c[t:u, u:] - dot6(near_row, out3, TN)
+                    for w in range(u, order, NB):
+                        a = w - u
                         c[w : w + NB, w:] = c[w : w + NB, w:] - dot6(
-                            out[:, w - t : w - t + NB], out[:, w - t :], TN
+                            [y[:, a : a + NB] for y in out3], [y[:, a:] for y in out3], TN
                         )
 
+            else:
+                m[o:t, :] = dot6(inverse, split3(c[o:t, order:]), NN)
             for lv, jj in ((0, 0), (0, 1), (0, 2), (0, 3), (1, 2), (2, 1)):
-
-                @pl.when((level == lv) & (j == jj))
-                def _(lv=lv, jj=jj):
-                    hook(lv, jj)
-
-            return carry
-
-        lax.fori_loop(0, steps, step, 0)
+                if jj == j:
+
+                    @pl.when(level == lv)
+                    def _(lv=lv, jj=jj):
+                        hook(lv, jj)
+
         for lv in range(3):
 
             @pl.when(level == lv)
@@ -501,8 +527,8 @@
         ],
         scratch_shapes=[
             vmem(4, rows, r),
-            pltpu.VMEM((4, rows, r), BF16),
-            pltpu.VMEM((4, rows, r), BF16),
+            pltpu.VMEM((3, r, rows), BF16),
+            pltpu.VMEM((3, r, rows), BF16),
             vmem(4, most, r, r),
             vmem(4, most, hr, r),
             vmem(4, most, hr, r),
@@ -520,8 +546,12 @@
             vmem(hr, 2 * r),
             vmem(order, r),
             vmem(3, order, order),
+            vmem(3, order, order),
+            pltpu.VMEM((3, 3, order, order), BF16),
+            pltpu.VMEM((3, 3, order, order), BF16),
             vmem(order, 2 * order),
             vmem(NB, NB),
+            vmem(W, W // 8, 8, NB),
             vmem(order, order),
             vmem(order, 3 * r),
             vmem(r, 3 * r),
@@ -539,7 +569,7 @@
             dma((2, 3, 3)),
         ],
         compiler_params=pltpu.CompilerParams(
-            collective_id=0, has_side_effects=True, vmem_limit_bytes=56 << 20
+            collective_id=0, has_side_effects=True, vmem_limit_bytes=60 << 20
         ),
         name="mega",
     )(b3, b2, b1, rhs, leaf.reshape(rows // 128, 128), cpl3, cpl2, cpl1)

time: 124 us -> 117 us (0.944)
  Pallas kernels: 122 us -> 116 us
    pallas_call x1, Pallas kernels: 115 us -> 109 us  [mega(): pl.pallas_call(lambda *refs: mega_kernel(chips, *refs), in_specs=[hbm] *...]
where the time goes in v3:
time: 117 us
  Pallas kernels  116 us (99%)
    pallas_call x1, Pallas kernels, mega(): pl.pallas_call(lambda *refs: mega_kernel(chips, *refs), in_specs=[hbm] *...  109 us
    pallas_call x1, Pallas kernels, apply_update(): pl.pallas_call(apply_kernel, grid=(rows // tile,), in_specs=[block] * 4 +...  7.28 us

profile of v3, /device:TPU:1, one launch (start us, length us, event | category | flops | bytes accessed | tf_op | source)
XLA Modules:
  0.0 116.6 jit_solution(11598235209630669060)
XLA Ops:
  0.6 108.7 %mega.1 = (f32[768,256]{1,0:T(8,128)}, f32[16,512]{1,0:T(8,128)}, f32[8,512]{1,0:T(8,128)}, f32[4,512]{1,0:T(4,128)}) custom-call(f32[2048,256]{1,0:T(8,128)} %b3.1, f32[2048,256]{1,0:T(8,128)} %b2.1, f32[2048,256]{1,0:T(8,128)} %b1.1, f32[2048,256]{1,0:T(8,128)} %rhs.1, f32[16,128]{1,0:T(8,128)} %bitcast.2, f32[4,512,512]{2,1,0:T(8,128)} %refs_5_.1, ...), custom_call_target="tpu_custom_call" | custom-call | tf_op jit(solution)/shard_map/mega/pallas_call | solution.py:520
  109.3 7.3 %apply_update.1 = (f32[2048,256]{1,0:T(8,128)}, f32[16,512]{1,0:T(8,128)}, f32[8,512]{1,0:T(8,128)}, f32[4,512]{1,0:T(4,128)}) custom-call(f32[2048,256]{1,0:T(8,128)} %b3.1, f32[2048,256]{1,0:T(8,128)} %b2.1, f32[2048,256]{1,0:T(8,128)} %b1.1, f32[2048,256]{1,0:T(8,128)} %rhs.1, f32[4,4,128]{2,1,0:T(4,128)} %bitcast.3, f32[768,256]{1,0:T(8,128)} %get-tuple-element.8.x, ...), custom_call_target="tpu_custom_call" | custom-call | tf_op jit(solution)/shard_map/apply_update/pallas_call | solution.py:600

commit v4 on v3

--- a/solution.py
+++ b/solution.py
@@ -120,15 +120,15 @@
 
 
 GROUPS = (((0, 0),), ((0, 1), (1, 1)), ((0, 2), (1, 2), (2, 2)), ((0, 3), (1, 3), (2, 3)))
-ORDER = {(1, 0): 0, (2, 0): 1, (2, 1): 3, (3, 0): 2, (3, 1): 4}
+ORDER = {(2, 0): 0, (3, 0): 1, (2, 1): 2, (3, 1): 3}
 TILE = 512
 
 
 def mega_kernel(
     chips, b3, b2, b1, rhs, leaf, cpl3, cpl2, cpl1, x, core3, core2, core1,
-    raw, hi_t, lo_t, part, near, half, arrived, piece, far, pay, bag, g, q, s, h, q1, s1, tail, q2,
+    raw, hi_t, lo_t, part, near, half, arrived, piece, far, pay, bag, g, q, s, own_s, h, q1, rows_q1, rows_q1_tail, s1, tail, tail_in, q2, rows_q2, strip,
     coupling, turned, l_parts, lt_parts, c, work, spread, m, p, v3, v2, krows,
-    load_sem, near_sem, rs_sem, ag_sem, share_sem, far_sem, bag_sem, bshare_sem, ex_sem, exs_sem,
+    load_sem, near_sem, rs_sem, ag_sem, share_sem, far_sem, bag_sem, bshare_sem, ex_sem, exs_sem, wide_sem, s1_sem, tail_sem, last_sem,
 ):
     gx, gy, core, chip, other, sib = where_am_i()
     rows, r = b3.shape
@@ -151,7 +151,14 @@
     ]
     loads[0].start()
     peers = group_peers(chips)
-    everyone = peers + [(far_gx[1], gy), (far_gx[2], gy)]
+    beyond = {}
+    for level in (1, 2):
+        beyond[level] = [
+            (base, 2 * ((chip + d) % chips) + core)
+            for base in (far_gx[level], far_gx[level] + 1 - 2 * (gx % 2))
+            for d in range(chips)
+        ]
+    everyone = peers + beyond[1] + beyond[2]
     greet(everyone)
     for copy in loads[1:]:
         copy.start()
@@ -197,7 +204,7 @@
         )
         for i in range(1, 4)
     ]
-    bag_rows = [pr + (pr // 2) * (len(GROUPS[i]) - 1) for i in range(1, 4)]
+    bag_rows = [pr + pr // 2, pr, pr]
     gathers = [
         [
             remote(
@@ -255,16 +262,23 @@
         if i > 0:
             across[i - 1].start()
 
+    keep = pl.ds(pl.multiple_of(side * (pr // 2), pr // 2), pr // 2)
+
     def gather(i):
-        across[i - 1].wait_recv()
         pay[i - 1, 0:pr, :] = piece[i, 0]
-        keep = pl.ds(pl.multiple_of(side * (pr // 2), pr // 2), pr // 2)
-        for n in range(len(GROUPS[i]) - 1):
-            at = pr + n * (pr // 2)
-            pay[i - 1, at : at + pr // 2, :] = piece[i, n + 1, keep, :] + far[i, n, keep, :]
+        if i == 1:
+            across[0].wait_recv()
+            pay[0, pr:, :] = piece[1, 1, keep, :] + far[1, 0, keep, :]
         for copy in gathers[i - 1]:
             copy.start()
         bag[i - 1, side, core, chip, 0 : bag_rows[i - 1], :] = pay[i - 1, 0 : bag_rows[i - 1], :]
+
+    def keep_sums(i):
+        across[i - 1].wait_recv()
+        for n in range(2):
+            own_s[:, ORDER[i, n] * r : (ORDER[i, n] + 1) * r] = (
+                piece[i, n + 1, keep, :] + far[i, n, keep, :]
+            )
 
     def share(i):
         for copy in gathers[i - 1]:
@@ -276,12 +290,9 @@
         for copy in bag_shares[i - 1]:
             copy.wait_recv()
         q[:, (i - 1) * r : i * r] = bag[i - 1, :, :, :, 0:pr, :].reshape(order, r)
-        for n in range(len(GROUPS[i]) - 1):
-            at = pr + n * (pr // 2)
+        if i == 1:
             for t in range(2):
-                s[ORDER[i, n], :, t] = bag[i - 1, t, :, :, at : at + pr // 2, :].reshape(
-                    2 * chips, pr // 2, r
-                )
+                s[:, t] = bag[0, t, :, :, pr:, :].reshape(2 * chips, pr // 2, r)
 
     def swap(level, src, dst, n):
         return remote(src, dst, ex_sem.at[0, level, n], ex_sem.at[1, level, n], (far_gx[level], gy))
@@ -290,16 +301,36 @@
         return remote(ref, ref, exs_sem.at[0, level, n], exs_sem.at[1, level, n], partner)
 
     mine = pl.ds(pl.multiple_of(core * hr, hr), hr)
-    ex_g, ex_q, sh_g, sh_q = {}, {}, {}, {}
+    ex_g, sh_g, sh_q = {}, {}, {}
     for level, qs in ((1, q1), (2, q2)):
         to = pl.ds(pl.multiple_of(sides[level] * r + core * hr, hr), hr)
         come = pl.ds(pl.multiple_of((1 - sides[level]) * r + core * hr, hr), hr)
-        ex_g[level] = swap(level, h.at[level - 1, 0, mine, :], g.at[level, to, :], 0)
-        ex_q[level] = swap(level, qs.at[to, :], qs.at[to, :], 1)
+        ex_g[level] = swap(level, h.at[level - 1, mine, :], g.at[level, to, :], 0)
         sh_g[level] = pass_on(level, g.at[level, come, :], 0)
-        sh_q[level] = pass_on(level, qs.at[come, :], 1)
-    ex_s = swap(1, s1.at[mine, :], tail, 2)
-    sh_s = pass_on(1, s1.at[mine, :], 2)
+        sh_q[level] = [pass_on(level, qs.at[at, :], 1 + n) for n, at in enumerate((to, come))]
+    sh_s = pass_on(1, s1.at[mine, :], 3)
+    low = pl.multiple_of(chip * pr + side * (pr // 2), pr // 2)
+    eight = pl.ds(low, pr // 2)
+    s1_at = pl.ds(pl.multiple_of(core * hr + low, pr // 2), pr // 2)
+    q_at = {
+        level: pl.ds(pl.multiple_of(sides[level] * r + core * hr + low, pr // 2), pr // 2)
+        for level in (1, 2)
+    }
+    wide_q1 = [
+        remote(rows_q1, q1.at[q_at[1], :], wide_sem.at[0, d], wide_sem.at[1, d], peer)
+        for d, peer in enumerate(peers[1:] + beyond[1])
+    ]
+    wide_q2 = [
+        remote(rows_q2, q2.at[q_at[2], :], last_sem.at[0, d], last_sem.at[1, d], peer)
+        for d, peer in enumerate(peers[1:] + beyond[2])
+    ]
+    s1_gather = [
+        remote(tail.at[:, pl.ds(0, r)], s1.at[s1_at, :], s1_sem.at[0, d], s1_sem.at[1, d], peer)
+        for d, peer in enumerate(peers[1:])
+    ]
+    tail_swap = remote(
+        rows_q1_tail, tail_in, tail_sem.at[0], tail_sem.at[1], (far_gx[1], gy)
+    )
 
     def prepare(level):
         loads[4 + level].wait()
@@ -328,6 +359,7 @@
     scatter(3)
     gather(1)
     collect(2)
+    gather(2)
     prepare(0)
     for copy in g_shares:
         copy.wait_recv()
@@ -339,29 +371,39 @@
     )
     steps = order // NB
 
-    def receive_q(level):
-        ex_q[level].wait_recv()
-        sh_q[level].start()
-
     def hook(level, j):
         if (level, j) == (0, 0):
-            gather(2)
             collect(3)
+            gather(3)
+            keep_sums(2)
         elif (level, j) == (0, 1):
-            gather(3)
+            keep_sums(3)
             share(1)
         elif (level, j) == (0, 2):
             share(2)
         elif (level, j) == (0, 3):
             share(3)
             unpack(1)
+        elif (level, j) == (1, 0):
+            tail_swap.wait_recv()
+            tail[...] = rows_q1_tail[...] + tail_in[...]
+            for copy in s1_gather:
+                copy.start()
+            s1[s1_at, :] = tail[:, 0:r]
+        elif (level, j) == (1, 1):
+            for copy in wide_q1:
+                copy.wait_recv()
+            for copy in sh_q[1]:
+                copy.start()
         elif (level, j) == (1, 2):
-            receive_q(1)
-            ex_s.wait()
-            s1[mine, :] = s1[mine, :] + tail[...]
+            for copy in s1_gather:
+                copy.wait_recv()
             sh_s.start()
         elif (level, j) == (2, 1):
-            receive_q(2)
+            for copy in wide_q2:
+                copy.wait_recv()
+            for copy in sh_q[2]:
+                copy.start()
 
     def core_block(out, level, count):
         place = gx * 2 * chips + gy
@@ -381,25 +423,30 @@
     def column(i):
         return split2(p[:, i * r : (i + 1) * r])
 
+    def strip_of(i, right, count):
+        left = split2(p[:, pl.ds(pl.multiple_of(i * r + core * hr, hr), hr)])
+        strip[:, 0:count] = dot3(left, right, TN)
+
     def after(level):
         ms = split2(m[...])
         if level == 0:
             p[:, 0:r] = dot3(ms, split2(q[:, 0:r]), NN)
             p2 = column(0)
-            h[0, 0] = s[0].reshape(r, r) - dot3(p2, p2, TN)
+            h[0] = s[...].reshape(r, r) - dot3(p2, p2, TN)
             ex_g[1].start()
-            g[1, pl.ds(pl.multiple_of(sides[1] * r, r), r), :] = h[0, 0]
+            g[1, pl.ds(pl.multiple_of(sides[1] * r, r), r), :] = h[0]
             unpack(2)
             unpack(3)
             p[:, r:] = dot3(ms, split2(q[:, r:]), NN)
-            p1, pc = column(1), column(2)
-            at = pl.ds(pl.multiple_of(sides[1] * r, r), r)
-            q1[at, 0:r] = s[1].reshape(r, r) - dot3(p2, p1, TN)
-            q1[at, r:] = s[2].reshape(r, r) - dot3(p2, pc, TN)
-            ex_q[1].start()
-            s1[:, 0:r] = s[3].reshape(r, r) - dot3(p1, p1, TN)
-            s1[:, r:] = s[4].reshape(r, r) - dot3(p1, pc, TN)
-            ex_s.start()
+            right = split2(p[:, r:])
+            strip_of(1, right, 2 * r)
+            rows_q1_tail[...] = own_s[:, 2 * r :] - strip[eight, :]
+            tail_swap.start()
+            strip_of(0, right, 2 * r)
+            rows_q1[...] = own_s[:, 0 : 2 * r] - strip[eight, :]
+            for copy in wide_q1:
+                copy.start()
+            q1[q_at[1], :] = rows_q1[...]
             prepare(1)
             ex_g[1].wait_recv()
             sh_g[1].start()
@@ -407,16 +454,19 @@
             core_block(core3, 0, 16)
             sh_g[1].wait_recv()
         elif level == 1:
-            sh_q[1].wait_recv()
-            sh_s.wait_recv()
+            for copy in (*sh_q[1], sh_s):
+                copy.wait_recv()
             p[:, 0:r] = dot3(ms, split2(q1[:, 0:r]), NN)
             p1 = column(0)
-            h[1, 0] = s1[:, 0:r] - dot3(p1, p1, TN)
+            h[1] = s1[...] - dot3(p1, p1, TN)
             ex_g[2].start()
-            g[2, pl.ds(pl.multiple_of(sides[2] * r, r), r), :] = h[1, 0]
+            g[2, pl.ds(pl.multiple_of(sides[2] * r, r), r), :] = h[1]
             p[:, r : 2 * r] = dot3(ms, split2(q1[:, r:]), NN)
-            q2[pl.ds(pl.multiple_of(sides[2] * r, r), r), :] = s1[:, r:] - dot3(p1, column(1), TN)
-            ex_q[2].start()
+            strip_of(0, column(1), r)
+            rows_q2[...] = tail[:, r:] - strip[eight, 0:r]
+            for copy in wide_q2:
+                copy.start()
+            q2[q_at[2], :] = rows_q2[...]
             prepare(2)
             ex_g[2].wait_recv()
             sh_g[2].start()
@@ -424,7 +474,8 @@
             core_block(core2, 1, 8)
             sh_g[2].wait_recv()
         else:
-            sh_q[2].wait_recv()
+            for copy in sh_q[2]:
+                copy.wait_recv()
             x1 = dot3(own_of(2), split2(dot3(ms, split2(q2[...]), NN)), TN)
             t1 = split2(x1)
             x2 = v2[:, r:] - dot3(split2(v2[:, :r]), t1, NN)
@@ -479,7 +530,7 @@
 
             else:
                 m[o:t, :] = dot6(inverse, split3(c[o:t, order:]), NN)
-            for lv, jj in ((0, 0), (0, 1), (0, 2), (0, 3), (1, 2), (2, 1)):
+            for lv, jj in ((0, 0), (0, 1), (0, 2), (0, 3), (1, 0), (1, 1), (1, 2), (2, 1)):
                 if jj == j:
 
                     @pl.when(level == lv)
@@ -495,8 +546,8 @@
         return carry
 
     lax.fori_loop(0, 3, one_level, 0)
-    sends = [*nears, *g_gather, *g_shares, *across, ex_g[1], ex_g[2], ex_q[1], ex_q[2]]
-    sends += [sh_g[1], sh_g[2], sh_q[1], sh_q[2], sh_s]
+    sends = [*nears, *g_gather, *g_shares, *across, ex_g[1], ex_g[2], sh_g[1], sh_g[2], sh_s]
+    sends += [*sh_q[1], *sh_q[2], *wide_q1, *wide_q2, *s1_gather, tail_swap]
     for copies in (*scatters, *gathers, *bag_shares):
         sends += copies
     for copy in sends:
@@ -510,7 +561,7 @@
     hr = r // 2
     pr = hr // chips
     most = max(len(y) for y in GROUPS)
-    wide = pr + (pr // 2) * (most - 1)
+    wide = pr + pr // 2
     hbm = pl.BlockSpec(memory_space=pl.ANY)
     dma = pltpu.SemaphoreType.DMA
 
@@ -539,12 +590,18 @@
             vmem(3, 2, 2, chips, wide, r),
             vmem(3, order, r),
             vmem(order, 3 * r),
-            vmem(5, 2 * chips, 2, pr // 2, r),
-            vmem(2, 1, r, r),
+            vmem(2 * chips, 2, pr // 2, r),
+            vmem(pr // 2, 4 * r),
+            vmem(2, r, r),
             vmem(order, 2 * r),
-            vmem(r, 2 * r),
+            vmem(pr // 2, 2 * r),
+            vmem(pr // 2, 2 * r),
+            vmem(r, r),
+            vmem(pr // 2, 2 * r),
+            vmem(pr // 2, 2 * r),
+            vmem(order, r),
+            vmem(pr // 2, r),
             vmem(hr, 2 * r),
-            vmem(order, r),
             vmem(3, order, order),
             vmem(3, order, order),
             pltpu.VMEM((3, 3, order, order), BF16),
@@ -565,8 +622,12 @@
             dma((2, 4)),
             dma((2, 3, 2 * chips - 1)),
             dma((2, 3, 2)),
-            dma((2, 3, 3)),
-            dma((2, 3, 3)),
+            dma((2, 3, 1)),
+            dma((2, 3, 4)),
+            dma((2, 4 * chips - 1)),
+            dma((2, 2 * chips - 1)),
+            dma((2,)),
+            dma((2, 4 * chips - 1)),
         ],
         compiler_params=pltpu.CompilerParams(
             collective_id=0, has_side_effects=True, vmem_limit_bytes=60 << 20

time: 117 us -> 122 us (1.043)
  the two profiles are of different devices: /device:TPU:1 before, /device:TPU:25 now
where the time goes in v4:
time: 122 us
  Pallas kernels  121 us (99%)
    pallas_call x1, Pallas kernels, mega(): pl.pallas_call(lambda *refs: mega_kernel(chips, *refs), in_specs=[hbm] *...  114 us
    pallas_call x1, Pallas kernels, apply_update(): pl.pallas_call(apply_kernel, grid=(rows // tile,), in_specs=[block] * 4 +...  7.28 us

profile of v4, /device:TPU:25, one launch (start us, length us, event | category | flops | bytes accessed | tf_op | source)
XLA Modules:
  0.0 121.7 jit_solution(6703437187005967797)
XLA Ops:
  0.6 113.8 %mega.1 = (f32[768,256]{1,0:T(8,128)}, f32[16,512]{1,0:T(8,128)}, f32[8,512]{1,0:T(8,128)}, f32[4,512]{1,0:T(4,128)}) custom-call(f32[2048,256]{1,0:T(8,128)} %b3.1, f32[2048,256]{1,0:T(8,128)} %b2.1, f32[2048,256]{1,0:T(8,128)} %b1.1, f32[2048,256]{1,0:T(8,128)} %rhs.1, f32[16,128]{1,0:T(8,128)} %bitcast.2, f32[4,512,512]{2,1,0:T(8,128)} %refs_5_.1, ...), custom_call_target="tpu_custom_call" | custom-call | tf_op jit(solution)/shard_map/mega/pallas_call | solution.py:571
  114.4 7.3 %apply_update.1 = (f32[2048,256]{1,0:T(8,128)}, f32[16,512]{1,0:T(8,128)}, f32[8,512]{1,0:T(8,128)}, f32[4,512]{1,0:T(4,128)}) custom-call(f32[2048,256]{1,0:T(8,128)} %b3.1, f32[2048,256]{1,0:T(8,128)} %b2.1, f32[2048,256]{1,0:T(8,128)} %b1.1, f32[2048,256]{1,0:T(8,128)} %rhs.1, f32[4,4,128]{2,1,0:T(4,128)} %bitcast.3, f32[768,256]{1,0:T(8,128)} %get-tuple-element.8.x, ...), custom_call_target="tpu_custom_call" | custom-call | tf_op jit(solution)/shard_map/apply_update/pallas_call | solution.py:661

commit v5 on v3

--- a/solution.py
+++ b/solution.py
@@ -192,30 +192,27 @@
         g_shares.append(remote(at, at, share_sem.at[0, t], share_sem.at[1, t], partner))
     across = [
         remote(
-            piece.at[i, pl.ds(1, len(GROUPS[i]) - 1)], far.at[i, pl.ds(0, len(GROUPS[i]) - 1)],
+            piece.at[i, pl.ds(0, len(GROUPS[i]))], far.at[i, pl.ds(0, len(GROUPS[i]))],
             far_sem.at[0, i], far_sem.at[1, i], (sib, gy),
         )
         for i in range(1, 4)
     ]
-    bag_rows = [pr + (pr // 2) * (len(GROUPS[i]) - 1) for i in range(1, 4)]
+    bag_rows = [pr * (len(GROUPS[i]) + 1) for i in range(1, 4)]
     gathers = [
         [
             remote(
-                pay.at[i, pl.ds(0, n), :], bag.at[i, side, core, chip, pl.ds(0, n), :],
+                pay.at[i, pl.ds(0, n), :], bag.at[i, core, chip, pl.ds(0, n), :],
                 bag_sem.at[0, i, d], bag_sem.at[1, i, d], peer,
             )
-            for d, peer in enumerate(peers[1:])
+            for d, peer in enumerate(peers[1:chips])
         ]
         for i, n in enumerate(bag_rows)
     ]
     bag_shares = [
-        [
-            remote(
-                bag.at[i, t, core, :, pl.ds(0, n), :], bag.at[i, t, core, :, pl.ds(0, n), :],
-                bshare_sem.at[0, i, t], bshare_sem.at[1, i, t], partner,
-            )
-            for t in range(2)
-        ]
+        remote(
+            bag.at[i, core, :, pl.ds(0, n), :], bag.at[i, core, :, pl.ds(0, n), :],
+            bshare_sem.at[0, i], bshare_sem.at[1, i], partner,
+        )
         for i, n in enumerate(bag_rows)
     ]
 
@@ -257,31 +254,29 @@
 
     def gather(i):
         across[i - 1].wait_recv()
-        pay[i - 1, 0:pr, :] = piece[i, 0]
-        keep = pl.ds(pl.multiple_of(side * (pr // 2), pr // 2), pr // 2)
-        for n in range(len(GROUPS[i]) - 1):
-            at = pr + n * (pr // 2)
-            pay[i - 1, at : at + pr // 2, :] = piece[i, n + 1, keep, :] + far[i, n, keep, :]
+        own_at = pl.ds(pl.multiple_of(side * pr, pr), pr)
+        far_at = pl.ds(pl.multiple_of((1 - side) * pr, pr), pr)
+        pay[i - 1, own_at, :] = piece[i, 0]
+        pay[i - 1, far_at, :] = far[i, 0]
+        for n in range(1, len(GROUPS[i])):
+            pay[i - 1, (n + 1) * pr : (n + 2) * pr, :] = piece[i, n] + far[i, n]
         for copy in gathers[i - 1]:
             copy.start()
-        bag[i - 1, side, core, chip, 0 : bag_rows[i - 1], :] = pay[i - 1, 0 : bag_rows[i - 1], :]
+        bag[i - 1, core, chip, 0 : bag_rows[i - 1], :] = pay[i - 1, 0 : bag_rows[i - 1], :]
 
     def share(i):
         for copy in gathers[i - 1]:
             copy.wait_recv()
-        for copy in bag_shares[i - 1]:
-            copy.start()
+        bag_shares[i - 1].start()
 
     def unpack(i):
-        for copy in bag_shares[i - 1]:
-            copy.wait_recv()
-        q[:, (i - 1) * r : i * r] = bag[i - 1, :, :, :, 0:pr, :].reshape(order, r)
-        for n in range(len(GROUPS[i]) - 1):
-            at = pr + n * (pr // 2)
-            for t in range(2):
-                s[ORDER[i, n], :, t] = bag[i - 1, t, :, :, at : at + pr // 2, :].reshape(
-                    2 * chips, pr // 2, r
-                )
+        bag_shares[i - 1].wait_recv()
+        for t in range(2):
+            q[t * r : (t + 1) * r, (i - 1) * r : i * r] = bag[
+                i - 1, :, :, t * pr : (t + 1) * pr, :
+            ].reshape(r, r)
+        for n in range(1, len(GROUPS[i])):
+            s[ORDER[i, n - 1]] = bag[i - 1, :, :, (n + 1) * pr : (n + 2) * pr, :].reshape(r, r)
 
     def swap(level, src, dst, n):
         return remote(src, dst, ex_sem.at[0, level, n], ex_sem.at[1, level, n], (far_gx[level], gy))
@@ -291,12 +286,20 @@
 
     mine = pl.ds(pl.multiple_of(core * hr, hr), hr)
     ex_g, ex_q, sh_g, sh_q = {}, {}, {}, {}
+    ch = hr // 2
     for level, qs in ((1, q1), (2, q2)):
-        to = pl.ds(pl.multiple_of(sides[level] * r + core * hr, hr), hr)
-        come = pl.ds(pl.multiple_of((1 - sides[level]) * r + core * hr, hr), hr)
-        ex_g[level] = swap(level, h.at[level - 1, 0, mine, :], g.at[level, to, :], 0)
+        base = sides[level] * r + core * hr
+        away = (1 - sides[level]) * r + core * hr
+        to = pl.ds(pl.multiple_of(base, hr), hr)
+        come = pl.ds(pl.multiple_of(away, hr), hr)
+        ex_g[level], sh_g[level] = [], []
+        for n in range(2):
+            from_at = pl.ds(pl.multiple_of(core * hr + n * ch, ch), ch)
+            to_at = pl.ds(pl.multiple_of(base + n * ch, ch), ch)
+            come_at = pl.ds(pl.multiple_of(away + n * ch, ch), ch)
+            ex_g[level].append(swap(level, h.at[level - 1, 0, from_at, :], g.at[level, to_at, :], 3 * n))
+            sh_g[level].append(pass_on(level, g.at[level, come_at, :], 3 * n))
         ex_q[level] = swap(level, qs.at[to, :], qs.at[to, :], 1)
-        sh_g[level] = pass_on(level, g.at[level, come, :], 0)
         sh_q[level] = pass_on(level, qs.at[come, :], 1)
     ex_s = swap(1, s1.at[mine, :], tail, 2)
     sh_s = pass_on(1, s1.at[mine, :], 2)
@@ -357,6 +360,7 @@
             unpack(1)
         elif (level, j) == (1, 2):
             receive_q(1)
+        elif (level, j) == (1, 3):
             ex_s.wait()
             s1[mine, :] = s1[mine, :] + tail[...]
             sh_s.start()
@@ -386,43 +390,49 @@
         if level == 0:
             p[:, 0:r] = dot3(ms, split2(q[:, 0:r]), NN)
             p2 = column(0)
-            h[0, 0] = s[0].reshape(r, r) - dot3(p2, p2, TN)
-            ex_g[1].start()
+            h[0, 0] = s[0] - dot3(p2, p2, TN)
+            for copy in ex_g[1]:
+                copy.start()
             g[1, pl.ds(pl.multiple_of(sides[1] * r, r), r), :] = h[0, 0]
             unpack(2)
             unpack(3)
             p[:, r:] = dot3(ms, split2(q[:, r:]), NN)
             p1, pc = column(1), column(2)
             at = pl.ds(pl.multiple_of(sides[1] * r, r), r)
-            q1[at, 0:r] = s[1].reshape(r, r) - dot3(p2, p1, TN)
-            q1[at, r:] = s[2].reshape(r, r) - dot3(p2, pc, TN)
+            q1[at, 0:r] = s[1] - dot3(p2, p1, TN)
+            q1[at, r:] = s[2] - dot3(p2, pc, TN)
             ex_q[1].start()
-            s1[:, 0:r] = s[3].reshape(r, r) - dot3(p1, p1, TN)
-            s1[:, r:] = s[4].reshape(r, r) - dot3(p1, pc, TN)
+            s1[:, 0:r] = s[3] - dot3(p1, p1, TN)
+            s1[:, r:] = s[4] - dot3(p1, pc, TN)
             ex_s.start()
             prepare(1)
-            ex_g[1].wait_recv()
-            sh_g[1].start()
+            for come_in, hand_on in zip(ex_g[1], sh_g[1]):
+                come_in.wait_recv()
+                hand_on.start()
             v3[...] = dot3(own_of(0), split2(p[...]), TN)
             core_block(core3, 0, 16)
-            sh_g[1].wait_recv()
+            for copy in sh_g[1]:
+                copy.wait_recv()
         elif level == 1:
             sh_q[1].wait_recv()
-            sh_s.wait_recv()
             p[:, 0:r] = dot3(ms, split2(q1[:, 0:r]), NN)
             p1 = column(0)
+            sh_s.wait_recv()
             h[1, 0] = s1[:, 0:r] - dot3(p1, p1, TN)
-            ex_g[2].start()
+            for copy in ex_g[2]:
+                copy.start()
             g[2, pl.ds(pl.multiple_of(sides[2] * r, r), r), :] = h[1, 0]
             p[:, r : 2 * r] = dot3(ms, split2(q1[:, r:]), NN)
             q2[pl.ds(pl.multiple_of(sides[2] * r, r), r), :] = s1[:, r:] - dot3(p1, column(1), TN)
             ex_q[2].start()
             prepare(2)
-            ex_g[2].wait_recv()
-            sh_g[2].start()
+            for come_in, hand_on in zip(ex_g[2], sh_g[2]):
+                come_in.wait_recv()
+                hand_on.start()
             v2[...] = dot3(own_of(1), split2(p[:, 0 : 2 * r]), TN)
             core_block(core2, 1, 8)
-            sh_g[2].wait_recv()
+            for copy in sh_g[2]:
+                copy.wait_recv()
         else:
             sh_q[2].wait_recv()
             x1 = dot3(own_of(2), split2(dot3(ms, split2(q2[...]), NN)), TN)
@@ -479,7 +489,7 @@
 
             else:
                 m[o:t, :] = dot6(inverse, split3(c[o:t, order:]), NN)
-            for lv, jj in ((0, 0), (0, 1), (0, 2), (0, 3), (1, 2), (2, 1)):
+            for lv, jj in ((0, 0), (0, 1), (0, 2), (0, 3), (1, 2), (1, 3), (2, 1)):
                 if jj == j:
 
                     @pl.when(level == lv)
@@ -495,9 +505,9 @@
         return carry
 
     lax.fori_loop(0, 3, one_level, 0)
-    sends = [*nears, *g_gather, *g_shares, *across, ex_g[1], ex_g[2], ex_q[1], ex_q[2]]
-    sends += [sh_g[1], sh_g[2], sh_q[1], sh_q[2], sh_s]
-    for copies in (*scatters, *gathers, *bag_shares):
+    sends = [*nears, *g_gather, *g_shares, *across, *ex_g[1], *ex_g[2], ex_q[1], ex_q[2]]
+    sends += [*sh_g[1], *sh_g[2], sh_q[1], sh_q[2], sh_s, *bag_shares]
+    for copies in (*scatters, *gathers):
         sends += copies
     for copy in sends:
         copy.wait_send()
@@ -510,7 +520,7 @@
     hr = r // 2
     pr = hr // chips
     most = max(len(y) for y in GROUPS)
-    wide = pr + (pr // 2) * (most - 1)
+    wide = pr * (most + 1)
     hbm = pl.BlockSpec(memory_space=pl.ANY)
     dma = pltpu.SemaphoreType.DMA
 
@@ -534,12 +544,12 @@
             vmem(4, most, hr, r),
             vmem(4, chips - 1, most, pr, r),
             vmem(4, most, pr, r),
-            vmem(4, most - 1, pr, r),
+            vmem(4, most, pr, r),
             vmem(3, wide, r),
-            vmem(3, 2, 2, chips, wide, r),
+            vmem(3, 2, chips, wide, r),
             vmem(3, order, r),
             vmem(order, 3 * r),
-            vmem(5, 2 * chips, 2, pr // 2, r),
+            vmem(5, r, r),
             vmem(2, 1, r, r),
             vmem(order, 2 * r),
             vmem(r, 2 * r),
@@ -563,10 +573,10 @@
             dma((2, 2 * chips - 1)),
             dma((2, 2)),
             dma((2, 4)),
-            dma((2, 3, 2 * chips - 1)),
-            dma((2, 3, 2)),
-            dma((2, 3, 3)),
-            dma((2, 3, 3)),
+            dma((2, 3, chips - 1)),
+            dma((2, 3)),
+            dma((2, 3, 4)),
+            dma((2, 3, 4)),
         ],
         compiler_params=pltpu.CompilerParams(
             collective_id=0, has_side_effects=True, vmem_limit_bytes=60 << 20

time: 117 us -> 111 us (0.949)
  Pallas kernels: 116 us -> 110 us
    pallas_call x1, Pallas kernels: 109 us -> 103 us  [mega(): pl.pallas_call(lambda *refs: mega_kernel(chips, *refs), in_specs=[hbm] *...]
where the time goes in v5:
time: 111 us
  Pallas kernels  110 us (99%)
    pallas_call x1, Pallas kernels, mega(): pl.pallas_call(lambda *refs: mega_kernel(chips, *refs), in_specs=[hbm] *...  103 us
    pallas_call x1, Pallas kernels, apply_update(): pl.pallas_call(apply_kernel, grid=(rows // tile,), in_specs=[block] * 4 +...  7.27 us

profile of v5, /device:TPU:1, one launch (start us, length us, event | category | flops | bytes accessed | tf_op | source)
XLA Modules:
  0.0 111.0 jit_solution(10162963243520015467)
XLA Ops:
  0.6 103.1 %mega.1 = (f32[768,256]{1,0:T(8,128)}, f32[16,512]{1,0:T(8,128)}, f32[8,512]{1,0:T(8,128)}, f32[4,512]{1,0:T(4,128)}) custom-call(f32[2048,256]{1,0:T(8,128)} %b3.1, f32[2048,256]{1,0:T(8,128)} %b2.1, f32[2048,256]{1,0:T(8,128)} %b1.1, f32[2048,256]{1,0:T(8,128)} %rhs.1, f32[16,128]{1,0:T(8,128)} %bitcast.2, f32[4,512,512]{2,1,0:T(8,128)} %refs_5_.1, ...), custom_call_target="tpu_custom_call" | custom-call | tf_op jit(solution)/shard_map/mega/pallas_call | solution.py:530
  103.7 7.3 %apply_update.1 = (f32[2048,256]{1,0:T(8,128)}, f32[16,512]{1,0:T(8,128)}, f32[8,512]{1,0:T(8,128)}, f32[4,512]{1,0:T(4,128)}) custom-call(f32[2048,256]{1,0:T(8,128)} %b3.1, f32[2048,256]{1,0:T(8,128)} %b2.1, f32[2048,256]{1,0:T(8,128)} %b1.1, f32[2048,256]{1,0:T(8,128)} %rhs.1, f32[4,4,128]{2,1,0:T(4,128)} %bitcast.3, f32[768,256]{1,0:T(8,128)} %get-tuple-element.8.x, ...), custom_call_target="tpu_custom_call" | custom-call | tf_op jit(solution)/shard_map/apply_update/pallas_call | solution.py:610

commit v6 on v5

--- a/solution.py
+++ b/solution.py
@@ -153,8 +153,6 @@
     peers = group_peers(chips)
     everyone = peers + [(far_gx[1], gy), (far_gx[2], gy)]
     greet(everyone)
-    for copy in loads[1:]:
-        copy.start()
     root = jnp.sqrt(leaf[...]).T
 
     nears = [
@@ -218,6 +216,8 @@
 
     def local(i):
         loads[i].wait()
+        for copy in (loads[1:4], loads[4:], [], [])[i]:
+            copy.start()
         n = len(GROUPS[i])
         for t in range(tiles):
             at = slice(t * TILE, (t + 1) * TILE)
@@ -406,10 +406,10 @@
             s1[:, r:] = s[4] - dot3(p1, pc, TN)
             ex_s.start()
             prepare(1)
+            v3[...] = dot3(own_of(0), split2(p[...]), TN)
             for come_in, hand_on in zip(ex_g[1], sh_g[1]):
                 come_in.wait_recv()
                 hand_on.start()
-            v3[...] = dot3(own_of(0), split2(p[...]), TN)
             core_block(core3, 0, 16)
             for copy in sh_g[1]:
                 copy.wait_recv()
@@ -426,10 +426,10 @@
             q2[pl.ds(pl.multiple_of(sides[2] * r, r), r), :] = s1[:, r:] - dot3(p1, column(1), TN)
             ex_q[2].start()
             prepare(2)
+            v2[...] = dot3(own_of(1), split2(p[:, 0 : 2 * r]), TN)
             for come_in, hand_on in zip(ex_g[2], sh_g[2]):
                 come_in.wait_recv()
                 hand_on.start()
-            v2[...] = dot3(own_of(1), split2(p[:, 0 : 2 * r]), TN)
             core_block(core2, 1, 8)
             for copy in sh_g[2]:
                 copy.wait_recv()

time: 111 us -> 111 us (level)
  no operation moved by 1% of the time
where the time goes in v6:
time: 111 us
  Pallas kernels  110 us (99%)
    pallas_call x1, Pallas kernels, mega(): pl.pallas_call(lambda *refs: mega_kernel(chips, *refs), in_specs=[hbm] *...  103 us
    pallas_call x1, Pallas kernels, apply_update(): pl.pallas_call(apply_kernel, grid=(rows // tile,), in_specs=[block] * 4 +...  7.27 us

profile of v6, /device:TPU:1, one launch (start us, length us, event | category | flops | bytes accessed | tf_op | source)
XLA Modules:
  0.0 110.9 jit_solution(12006542489727711678)
XLA Ops:
  0.6 103.0 %mega.1 = (f32[768,256]{1,0:T(8,128)}, f32[16,512]{1,0:T(8,128)}, f32[8,512]{1,0:T(8,128)}, f32[4,512]{1,0:T(4,128)}) custom-call(f32[2048,256]{1,0:T(8,128)} %b3.1, f32[2048,256]{1,0:T(8,128)} %b2.1, f32[2048,256]{1,0:T(8,128)} %b1.1, f32[2048,256]{1,0:T(8,128)} %rhs.1, f32[16,128]{1,0:T(8,128)} %bitcast.2, f32[4,512,512]{2,1,0:T(8,128)} %refs_5_.1, ...), custom_call_target="tpu_custom_call" | custom-call | tf_op jit(solution)/shard_map/mega/pallas_call | solution.py:530
  103.6 7.3 %apply_update.1 = (f32[2048,256]{1,0:T(8,128)}, f32[16,512]{1,0:T(8,128)}, f32[8,512]{1,0:T(8,128)}, f32[4,512]{1,0:T(4,128)}) custom-call(f32[2048,256]{1,0:T(8,128)} %b3.1, f32[2048,256]{1,0:T(8,128)} %b2.1, f32[2048,256]{1,0:T(8,128)} %b1.1, f32[2048,256]{1,0:T(8,128)} %rhs.1, f32[4,4,128]{2,1,0:T(4,128)} %bitcast.3, f32[768,256]{1,0:T(8,128)} %get-tuple-element.8.x, ...), custom_call_target="tpu_custom_call" | custom-call | tf_op jit(solution)/shard_map/apply_update/pallas_call | solution.py:610
